TPU v7x, 256 devices: a whole 4x4x8 slice. The times are simulated.
256 devices in a mesh: seq: 32 (over z, x), head: 8 (over y, core).
Axes of the slice: x: 4, y: 4, z: 8, core: 2. Of those that a mesh axis runs over, the one named last changes fastest.
Arguments:
- tokens: bfloat16 [4096, 2048], P('seq'), may hold values from -6.5 to 6.5
- w_query: bfloat16 [2048, 2048], P(None, 'head'), may hold values from -0.125 to 0.125
- w_key: bfloat16 [2048, 4096], P(None, 'head'), may hold values from -0.125 to 0.125
- w_value: bfloat16 [2048, 4096], P(None, 'head'), may hold values from -0.125 to 0.125
- w_beta: bfloat16 [2048, 32], P(None, 'head'), may hold values from -0.150160646 to 0.150160646
- grad_out: bfloat16 [4096, 2048], P('seq', 'head'), may hold values from -6 to 6
Outputs:
- grad_tokens: bfloat16 [4096, 2048], P('seq', 'head')
- grad_w_query: float32 [2048, 2048], P('seq', 'head')
- grad_w_key: float32 [2048, 4096], P('seq', 'head')
- grad_w_value: float32 [2048, 4096], P('seq', 'head')
- grad_w_beta: float32 [2048, 32], P('seq', 'head')
All inputs are finite; a program needn't handle non-finite values.
Results may differ from a plain program's by a relative error of at most 0.015.
Values may be sent and summed in bfloat16 or wider, within the bound.
A program may use at most 64 MiB of HBM per device.

v0:
```python
import jax
import jax.numpy as jnp
from jax import lax
from jax.sharding import PartitionSpec as P

HEAD_SIZE = 128
NH = 2
SPAN = 64


highest = lax.Precision.HIGHEST
epsilon = 1e-06


def passed_along(array, axis, by):
    devices = lax.axis_size(axis)
    pairs = [(i, i + by) for i in range(devices) if 0 <= i + by < devices]
    return lax.ppermute(array, axis, pairs)


def product(left, right):
    return jnp.matmul(left, right, precision=highest)


def batch_product(left, right):
    return jnp.einsum("hij,hjk->hik", left, right, precision=highest)


def normalize(matrix):
    return matrix * lax.rsqrt(jnp.sum(matrix * matrix, axis=-1, keepdims=True) + epsilon)


def block_weights(key_rows, beta_rows):
    step_count = key_rows.shape[0]
    key_gram = beta_rows[:, None] * product(key_rows, key_rows.T)
    system = jnp.eye(step_count, dtype=key_gram.dtype) + jnp.tril(key_gram, -1)
    return lax.linalg.triangular_solve(
        system, jnp.diag(beta_rows), left_side=True, lower=True, unit_diagonal=True
    )


def span_update(carry_state, pieces):
    query_rows, key_rows, value_rows, beta_rows = pieces
    step_count = key_rows.shape[0]
    row_count = query_rows.shape[0]
    weighting = block_weights(key_rows, beta_rows)
    w_rows = product(weighting, key_rows)
    new_values = product(weighting, value_rows) - product(w_rows, carry_state)
    column_token = lax.broadcasted_iota(jnp.int32, (row_count, step_count), 1) // (
        step_count // row_count
    )
    row_token = lax.broadcasted_iota(jnp.int32, (row_count, step_count), 0)
    scores = jnp.where(column_token <= row_token, product(query_rows, key_rows.T), 0.0)
    outputs = product(query_rows, carry_state) + product(scores, new_values)
    return (carry_state + product(key_rows.T, new_values), outputs)


def span_map(carry, pieces):
    transition, shifted = carry
    key_rows, value_rows, beta_rows = pieces
    weighting = block_weights(key_rows, beta_rows)
    w_rows = product(weighting, key_rows)
    new_values = product(weighting, value_rows) - product(w_rows, shifted)
    next_shift = shifted + product(key_rows.T, new_values)
    next_transition = transition - product(key_rows.T, product(w_rows, transition))
    return ((next_transition, next_shift), None)


def prepared(proj_query, proj_key, proj_value, proj_beta, head_count):
    row_count = proj_query.shape[0]
    queries = normalize(proj_query.reshape(row_count, head_count, HEAD_SIZE)).transpose(1, 0, 2)
    key_rows = (
        normalize(proj_key.reshape(row_count, head_count, NH, HEAD_SIZE))
        .transpose(1, 0, 2, 3)
        .reshape(head_count, row_count * NH, HEAD_SIZE)
    )
    value_rows = (
        proj_value.reshape(row_count, head_count, NH, HEAD_SIZE)
        .transpose(1, 0, 2, 3)
        .reshape(head_count, row_count * NH, HEAD_SIZE)
    )
    beta_rows = (
        (2.0 * jax.nn.sigmoid(proj_beta))
        .reshape(row_count, head_count, NH)
        .transpose(1, 0, 2)
        .reshape(head_count, row_count * NH)
    )
    return (queries, key_rows, value_rows, beta_rows)


def head_run(start_state, query_rows, key_rows, value_rows, beta_rows):
    blocks = query_rows.shape[0] // SPAN
    pieces = (
        query_rows.reshape(blocks, SPAN, HEAD_SIZE),
        key_rows.reshape(blocks, SPAN * NH, HEAD_SIZE),
        value_rows.reshape(blocks, SPAN * NH, HEAD_SIZE),
        beta_rows.reshape(blocks, SPAN * NH),
    )
    end_state, outputs = lax.scan(span_update, start_state, pieces)
    return (end_state, outputs.reshape(blocks * SPAN, HEAD_SIZE))


def head_map(key_rows, value_rows, beta_rows):
    blocks = key_rows.shape[0] // (SPAN * NH)
    pieces = (
        key_rows.reshape(blocks, SPAN * NH, HEAD_SIZE),
        value_rows.reshape(blocks, SPAN * NH, HEAD_SIZE),
        beta_rows.reshape(blocks, SPAN * NH),
    )
    start = (jnp.eye(HEAD_SIZE, dtype=jnp.float32), jnp.zeros((HEAD_SIZE, HEAD_SIZE), jnp.float32))
    result, unused = lax.scan(span_map, start, pieces)
    return result


def recurrence(proj_query, proj_key, proj_value, proj_beta, start_state):
    head_count = start_state.shape[0]
    row_count = proj_query.shape[0]
    queries, key_rows, value_rows, beta_rows = prepared(
        proj_query, proj_key, proj_value, proj_beta, head_count
    )
    end_states, outputs = jax.vmap(head_run)(start_state, queries, key_rows, value_rows, beta_rows)
    return (outputs.transpose(1, 0, 2).reshape(row_count, head_count * HEAD_SIZE), end_states)


def per_device(tokens, w_query, w_key, w_value, w_beta, grad_out):
    weights = (w_query, w_key, w_value, w_beta)
    proj_query = jnp.dot(tokens, w_query, preferred_element_type=jnp.float32)
    proj_key = jnp.dot(tokens, w_key, preferred_element_type=jnp.float32)
    proj_value = jnp.dot(tokens, w_value, preferred_element_type=jnp.float32)
    proj_beta = jnp.dot(tokens, w_beta, preferred_element_type=jnp.float32)
    head_count = w_query.shape[1] // HEAD_SIZE
    zero_state = jnp.zeros((head_count, HEAD_SIZE, HEAD_SIZE), jnp.float32)
    cotangent = grad_out.astype(jnp.float32)
    queries, key_rows, value_rows, beta_rows = prepared(
        proj_query, proj_key, proj_value, proj_beta, head_count
    )
    transition, local_shift = jax.vmap(head_map)(key_rows, value_rows, beta_rows)
    transition_t = jnp.swapaxes(transition, 1, 2)

    def outputs_from(start_state):
        return recurrence(proj_query, proj_key, proj_value, proj_beta, start_state)[0]

    unused_outputs, output_pull = jax.vjp(outputs_from, zero_state)
    local_adjoint = output_pull(cotangent)[0]
    seq_count = lax.axis_size("seq")

    def advance(token_position, start_state):
        return passed_along(batch_product(transition, start_state) + local_shift, "seq", 1)

    def retreat(token_position, end_adjoint):
        return passed_along(batch_product(transition_t, end_adjoint) + local_adjoint, "seq", -1)

    start_state = lax.fori_loop(0, seq_count - 1, advance, zero_state)
    end_adjoint = lax.fori_loop(0, seq_count - 1, retreat, zero_state)
    final_result, full_pull = jax.vjp(
        recurrence, proj_query, proj_key, proj_value, proj_beta, start_state
    )
    gradients = full_pull((cotangent, end_adjoint))
    rounded = tuple((gradient.astype(jnp.bfloat16) for gradient in gradients[:4]))
    grad_all = jnp.concatenate(rounded, axis=1)
    summed = lax.psum_scatter(
        lax.dot_general(
            tokens, grad_all, (((0,), (0,)), ((), ())), preferred_element_type=jnp.float32
        ).astype(jnp.bfloat16),
        "seq",
        scatter_dimension=0,
        tiled=True,
    ).astype(jnp.float32)
    first_cut = rounded[0].shape[1]
    second_cut = first_cut + rounded[1].shape[1]
    third_cut = second_cut + rounded[2].shape[1]
    input_term = lax.dot_general(
        rounded[0], weights[0], (((1,), (1,)), ((), ())), preferred_element_type=jnp.float32
    )
    input_term = input_term + lax.dot_general(
        rounded[1], weights[1], (((1,), (1,)), ((), ())), preferred_element_type=jnp.float32
    )
    input_term = input_term + lax.dot_general(
        rounded[2], weights[2], (((1,), (1,)), ((), ())), preferred_element_type=jnp.float32
    )
    input_term = input_term + lax.dot_general(
        rounded[3], weights[3], (((1,), (1,)), ((), ())), preferred_element_type=jnp.float32
    )
    grad_tokens = lax.psum_scatter(
        input_term.astype(jnp.bfloat16), "head", scatter_dimension=1, tiled=True
    )
    return (
        grad_tokens,
        summed[:, :first_cut],
        summed[:, first_cut:second_cut],
        summed[:, second_cut:third_cut],
        summed[:, third_cut:],
    )


def solution(mesh):
    in_specs = (
        P("seq", None),
        P(None, "head"),
        P(None, "head"),
        P(None, "head"),
        P(None, "head"),
        P("seq", "head"),
    )
    out_specs = (
        P("seq", "head"),
        P("seq", "head"),
        P("seq", "head"),
        P("seq", "head"),
        P("seq", "head"),
    )
    return jax.shard_map(
        per_device, mesh=mesh, in_specs=in_specs, out_specs=out_specs, check_vma=False
    )
```

profile of v0, /device:TPU:32, one launch (start us, length us, event | category | flops | bytes accessed | tf_op | source)
XLA Modules:
  0.0 1260.1 jit_solution(4720368216157703193)
XLA Ops:
  24.6 49.5 %while.130 = (s32[]{:T(128)}, f32[2,128,128]{2,1,0:T(8,128)S(1)}, f32[2,128,128]{2,1,0:T(8,128)S(1)}, f32[2,2,128,128]{3,2,1,0:T(8,128)S(1)}, f32[2,2,128]{2,1,0...) while((s32[]{:T(128)}, f32[2,128,128]{2,1,0:T(8,128)S(1)}, ...), condition=%wide.region_2.4_spmd.clone, body=%wide.region_1.3_spmd.clone.sunk | while | flops 403112064 | bytes 3613852 | solution.py:111
  26.7 19.7 %custom-call.24 = f32[2,1,128,128]{2,3,1,0:T(8,128)S(1)} custom-call(f32[2,1,128,128]{3,2,1,0:T(8,128)S(1)} %fusion.523), custom_call_target="InvertDiagBlocksLowerTriangular" | custom-call | tf_op jit(solution)/shard_map/vmap()/while/body/eval_jaxpr/triangular_solve/custom-call.1 | solution.py:37
  51.3 19.7 %custom-call.24 = f32[2,1,128,128]{2,3,1,0:T(8,128)S(1)} custom-call(f32[2,1,128,128]{3,2,1,0:T(8,128)S(1)} %fusion.523), custom_call_target="InvertDiagBlocksLowerTriangular" | custom-call | tf_op jit(solution)/shard_map/vmap()/while/body/eval_jaxpr/triangular_solve/custom-call.1 | solution.py:37
  77.5 51.5 %while.127 = (s32[]{:T(128)}, f32[2,2,128,128]{3,2,1,0:T(8,128)}, f32[2,2,64,128]{3,2,1,0:T(8,128)}, f32[2,2,128,128]{2,3,1,0:T(8,128)}, f32[2,2,128]{2,1,0:T(2,...) while((s32[]{:T(128)}, f32[2,2,128,128]{3,2,1,0:T(8,128)}, ...), condition=%wide.region_5.7_spmd.clone, body=%wide.region_4.6_spmd.clone.sunk | while | flops 176455808 | bytes 1789597 | solution.py:99
  79.2 19.7 %custom-call.21 = f32[2,1,128,128]{2,3,1,0:T(8,128)S(1)} custom-call(f32[2,1,128,128]{3,2,1,0:T(8,128)S(1)} %fusion.436), custom_call_target="InvertDiagBlocksLowerTriangular" | custom-call | tf_op jit(solution)/shard_map/jvp(vmap())/while/body/eval_jaxpr/triangular_solve/custom-call.1 | solution.py:37
  104.9 19.7 %custom-call.21 = f32[2,1,128,128]{2,3,1,0:T(8,128)S(1)} custom-call(f32[2,1,128,128]{3,2,1,0:T(8,128)S(1)} %fusion.436), custom_call_target="InvertDiagBlocksLowerTriangular" | custom-call | tf_op jit(solution)/shard_map/jvp(vmap())/while/body/eval_jaxpr/triangular_solve/custom-call.1 | solution.py:37
  137.3 292.1 %while.126 = (s32[]{:T(128)}, f32[2,128,128]{2,1,0:T(8,128)S(1)}, f32[2,128,128]{2,1,0:T(8,128)S(1)}, f32[2,128,128]{2,1,0:T(8,128)S(1)}, s32[]{:T(128)}) while((s32[]{:T(128)}, f32[2,128,128]{2,1,0:T(8,128)S(1)}, f32[2,128,128]{2,1,0:T(8,128)S(1)}, f32[2,128,128]{2,1,0:T(8,128)S(1)}, s32[]{:T(128)}) %tuple.288), condition=%wide.region_11.13_spmd, body=%wide.region_10.12_spmd.sunk | while | flops 50364416 | bytes 1048677 | solution.py:153
  435.2 63.5 %while.128 = (s32[]{:T(128)}, f32[2,128,128]{2,1,0:T(8,128)S(1)}, f32[2,2,128,128]{2,3,1,0:T(8,128)}, f32[2,2,128,128]{3,2,1,0:T(8,128)}, f32[2,2,128,1]{2,1,3,0...) while((s32[]{:T(128)}, f32[2,128,128]{2,1,0:T(8,128)S(1)}, ...), condition=%wide.region_13.15_spmd.clone, body=%wide.region_12.14_spmd.clone.sunk | while | flops 327614592 | bytes 4497137 | solution.py:99
  442.1 20.5 %custom-call.22 = f32[2,1,128,128]{2,3,1,0:T(8,128)S(1)} custom-call(f32[2,1,128,128]{3,2,1,0:T(8,128)} %add_bitcast_fusion.2), custom_call_target="InvertDiagBlocksLowerTriangular" | custom-call | tf_op jit(solution)/shard_map/jvp(vmap())/while/body/eval_jaxpr/triangular_solve/custom-call.1 | solution.py:37
  473.9 20.5 %custom-call.22 = f32[2,1,128,128]{2,3,1,0:T(8,128)S(1)} custom-call(f32[2,1,128,128]{3,2,1,0:T(8,128)} %add_bitcast_fusion.2), custom_call_target="InvertDiagBlocksLowerTriangular" | custom-call | tf_op jit(solution)/shard_map/jvp(vmap())/while/body/eval_jaxpr/triangular_solve/custom-call.1 | solution.py:37
  498.9 348.0 %while.125 = (s32[]{:T(128)}, f32[2,128,128]{2,1,0:T(8,128)S(1)}, f32[2,128,128]{2,1,0:T(8,128)S(1)}, f32[2,128,128]{2,1,0:T(8,128)S(1)}, s32[]{:T(128)}) while((s32[]{:T(128)}, f32[2,128,128]{2,1,0:T(8,128)S(1)}, f32[2,128,128]{2,1,0:T(8,128)S(1)}, f32[2,128,128]{2,1,0:T(8,128)S(1)}, s32[]{:T(128)}) %tuple.285), condition=%wide.region_9.11_spmd, body=%wide.region_8.10_spmd.sunk | while | flops 50364416 | bytes 1048677 | solution.py:154
  596.3 10.1 collective-permute-done
  609.3 8.8 collective-permute-done
  621.0 8.8 collective-permute-done
  678.2 9.0 collective-permute-done
  690.1 9.2 collective-permute-done
  702.2 9.0 collective-permute-done
  725.4 8.9 collective-permute-done
  759.3 9.0 collective-permute-done
  848.2 78.6 %while.129 = (s32[]{:T(128)}, f32[2,128,128]{2,1,0:T(8,128)S(1)}, f32[2,2,64,128]{3,2,0,1:T(8,128)S(1)}, f32[2,2,128,128]{3,2,0,1:T(8,128)}, bf16[2,2,128,128]{3...) while((s32[]{:T(128)}, f32[2,128,128]{2,1,0:T(8,128)S(1)}, ...), condition=%wide.region_17.20_spmd.clone.clone, body=%wide.region_14.19_spmd.clone.clone.sunk | while | flops 806076288 | bytes 15246945 | solution.py:99
  854.1 20.3 %custom-call.23 = f32[2,1,128,128]{2,3,1,0:T(8,128)} custom-call(f32[2,1,128,128]{3,2,1,0:T(8,128)S(1)} %fusion.497), custom_call_target="InvertDiagBlocksLowerTriangular" | custom-call | tf_op jit(solution)/shard_map/transpose(jvp(vmap()))/while/body/eval_jaxpr/triangular_solve/custom-call.0 | solution.py:37
  893.4 20.3 %custom-call.23 = f32[2,1,128,128]{2,3,1,0:T(8,128)} custom-call(f32[2,1,128,128]{3,2,1,0:T(8,128)S(1)} %fusion.497), custom_call_target="InvertDiagBlocksLowerTriangular" | custom-call | tf_op jit(solution)/shard_map/transpose(jvp(vmap()))/while/body/eval_jaxpr/triangular_solve/custom-call.0 | solution.py:37
  952.3 264.9 %reduce-scatter.7.cloned.1.call-done = bf16[64,1284]{1,0:T(8,128)(2,1)} async-done(((bf16[2048,1284]{1,0:T(8,128)(2,1)}), bf16[64,1284]{1,0:T(8,128)(2,1)}) %reduce-scatter.7.cloned.1.call-update) | async-done | bytes 164368
  1221.2 32.1 %reduce-scatter.5.cloned.1.call-done = bf16[128,256]{1,0:T(8,128)(2,1)} async-done(((bf16[128,2048]{1,0:T(8,128)(2,1)}), bf16[128,256]{1,0:T(8,128)(2,1)}) %reduce-scatter.5.cloned.1.call-update) | async-done | bytes 65552 | tf_op jit(solution)/shard_map/reduce_scatter | solution.py:184
  (496 shorter events, 721.5 us)
Async XLA Ops:
  7.2 1210.0 %reduce-scatter.7.cloned.1.call-start = ((), (), s32[]{:S(2)}) async-start(), calls=%async_computation.3 | async-start | bytes 5947392
  335.5 10.2 collective-permute-start.1
  558.0 10.6 collective-permute-start
  569.6 10.8 collective-permute-start
  581.3 11.4 collective-permute-start
  593.6 12.8 %collective-permute-start = (f32[2,128,128]{2,1,0:T(8,128)}, f32[2,128,128]{2,1,0:T(8,128)S(1)}, u32[]{:S(2)}, u32[]{:S(2)}) collective-permute-start(f32[2,128,128]{2,1,0:T(8,128)} %convolution_add_fusion.20), channel_id=1, source_target_pairs={{8,0},{16,8},{24,16},{32,24},{40,32},{48,40},{56,48},{64,56},{72,6... | collective-permute-start | bytes 393224 | tf_op jit(solution)/shard_map/while/body/eval_jaxpr/ppermute | solution.py:18
  607.4 10.8 collective-permute-start
  619.1 10.8 collective-permute-start
  630.7 10.7 collective-permute-start
  642.4 10.4 collective-permute-start
  664.7 10.6 collective-permute-start
  676.2 11.0 collective-permute-start
  688.1 11.2 collective-permute-start
  700.2 10.9 collective-permute-start
  712.0 10.5 collective-permute-start
  723.5 10.8 collective-permute-start
  746.0 10.4 collective-permute-start
  757.3 10.9 collective-permute-start
  780.0 10.1 collective-permute-start
  801.8 10.4 collective-permute-start
  813.1 10.6 collective-permute-start
  824.6 10.7 collective-permute-start
  836.2 10.7 collective-permute-start
  946.9 306.3 %reduce-scatter.5.cloned.1.call-start = ((), (), s32[]{:S(2)}) async-start(), calls=%async_computation.2 | async-start | bytes 589824 | tf_op jit(solution)/shard_map/reduce_scatter | solution.py:184
  (88 other events, 1349.2 us)
Sparse Core Ops, SparseCore 0:
  947.1 270.0 reduce-scatter.6
  1220.2 32.9 reduce-scatter.4
where the time goes:
time: 1260 us
  waiting for transfers between devices  747 us (59%)
  other arithmetic  176 us (14%)
  starting transfers between devices  152 us (12%)
  matrix products  119 us (9%)
  local copies, waits for them, and re-layouts  49.4 us (4%)
  between operations  14.5 us (1%)
    ppermute x62, waiting for transfers between devices, passed_along(): return lax.ppermute(array, axis, pairs)  450 us
    unnamed x3, waiting for transfers between devices  265 us
    another operation x28, other arithmetic, block_weights(): lax.linalg.triangular_solve(system, jnp.diag(beta_rows), left_side=True,...  164 us
    ppermute x62, starting transfers between devices, passed_along(): return lax.ppermute(array, axis, pairs)  152 us
    dot_general x72, matrix products, product(): return jnp.matmul(left, right, precision=highest)  55.3 us
    dot_general x62, matrix products, batch_product(): return jnp.einsum('hij,hjk->hik', left, right, precision=highest)  37.2 us
    reduce_scatter x1, waiting for transfers between devices, per_device(): lax.psum_scatter(input_term.astype(jnp.bfloat16), 'head', scatter_dimensi...  32.1 us
  transfers between devices with their start and end apart: 64, of which 64 were waited for; matrix products, arithmetic and copies ran while one was open for 1% of the time, Pallas kernels for 0%

commit v1 on v0

v1 whole, which is shorter than its diff:
```python
import functools

import jax
import jax.numpy as jnp
from jax import lax
from jax.experimental import pallas as pl
from jax.experimental.pallas import tpu as pltpu
from jax.sharding import PartitionSpec as P

HEAD_SIZE = 128
NH = 2
XN = 4
EPS = 1e-6
MESH = pl.DeviceIdType.MESH
F32 = jnp.float32
BF16 = jnp.bfloat16

NN = ((1,), (0,))
NT = ((1,), (1,))
TN = ((0,), (0,))


def dg(left, right, dims):
    return lax.dot_general(left, right, (dims, ((), ())), preferred_element_type=F32)


def parts(array):
    if isinstance(array, tuple):
        return array
    if array.dtype == BF16:
        return (array,)
    high = array.astype(BF16)
    return (high, (array - high.astype(F32)).astype(BF16))


def mm(left, right, dims=NN):
    left, right = parts(left), parts(right)
    total = dg(left[0], right[0], dims)
    if len(right) > 1:
        total = total + dg(left[0], right[1], dims)
    if len(left) > 1:
        total = total + dg(left[1], right[0], dims)
    return total


def order_masks(tokens):
    rows = NH * tokens
    row = lax.broadcasted_iota(jnp.int32, (rows, rows), 0)
    col = lax.broadcasted_iota(jnp.int32, (rows, rows), 1)
    row_token, col_token = row & (tokens - 1), col & (tokens - 1)
    row_step, col_step = row >= tokens, col >= tokens
    return row, col, row_token, col_token, row_step, col_step


def score_mask(tokens):
    row = lax.broadcasted_iota(jnp.int32, (tokens, NH * tokens), 0)
    col = lax.broadcasted_iota(jnp.int32, (tokens, NH * tokens), 1)
    return (col & (tokens - 1)) <= row


def unit(matrix):
    scale = lax.rsqrt(jnp.sum(matrix * matrix, axis=-1, keepdims=True) + EPS)
    return matrix * scale, scale


def front_kernel(
    heads,
    tokens_ref,
    wq_ref,
    wk_ref,
    wv_ref,
    wb_ref,
    go_ref,
    a_ref,
    bt_ref,
    lt_ref,
    q_ref,
    k_ref,
    v_ref,
    u_ref,
    w_ref,
    x_ref,
    pg_ref,
    col_ref,
):
    size = HEAD_SIZE
    tok = tokens_ref[...]
    count = tok.shape[0]
    pq = dg(tok, wq_ref[...], NN)
    pk = dg(tok, wk_ref[...], NN)
    pv = dg(tok, wv_ref[...], NN)
    pb = dg(tok, wb_ref[...], NN)
    beta_all = 2.0 * jax.nn.sigmoid(pb)
    row, col, row_token, col_token, row_step, col_step = order_masks(count)
    strict = (col_token < row_token) | ((col_token == row_token) & row_step & ~col_step)
    smask = score_mask(count)
    eye = jnp.where(row == col, 1.0, 0.0)
    keys, values, betas, systems, inverses = [], [], [], [], []
    for h in range(heads):
        base = h * NH * size
        both = jnp.concatenate([pk[:, base : base + size], pk[:, base + size : base + 2 * size]], axis=0)
        key, key_scale = unit(both)
        value = jnp.concatenate([pv[:, base : base + size], pv[:, base + size : base + 2 * size]], axis=0)
        beta = jnp.concatenate([beta_all[:, 2 * h : 2 * h + 1], beta_all[:, 2 * h + 1 : 2 * h + 2]], axis=0)
        k_ref[h] = key
        v_ref[h] = value
        col_ref[h, :, 0:1] = beta
        col_ref[h, :, 1:2] = key_scale
        gram = mm(key, key, NT)
        system = jnp.where(strict, beta * gram, 0.0)
        keys.append(key)
        values.append(value)
        betas.append(beta)
        systems.append(system)
        inverses.append(eye - jnp.where(col_token == row_token, system, 0.0))
    level = 1
    while level < count:
        pick = ((row_token & (2 * level - 1)) >= level) & ((col_token | (2 * level - 1)) == (row_token | (2 * level - 1))) & (
            (col_token & (2 * level - 1)) < level
        )
        for h in range(heads):
            inverse = parts(inverses[h])
            inner = mm(jnp.where(pick, systems[h], 0.0), inverse)
            inverses[h] = inverses[h] - mm(inverse, inner)
        level *= 2
    small = jnp.where(
        lax.broadcasted_iota(jnp.int32, (size, size), 0) == lax.broadcasted_iota(jnp.int32, (size, size), 1), 1.0, 0.0
    )
    for h in range(heads):
        key, value, beta, inverse = keys[h], values[h], betas[h], inverses[h]
        x_ref[h] = inverse
        inverse = parts(inverse)
        w_rows = mm(inverse, beta * key)
        u_rows = mm(inverse, beta * value)
        query, query_scale = unit(pq[:, h * size : (h + 1) * size])
        go = go_ref[:, h * size : (h + 1) * size]
        key = parts(key)
        scores = jnp.where(smask, mm(query, key, NT), 0.0)
        pulled = mm(scores, go, TN)
        w_parts = parts(w_rows)
        a_ref[h] = small - mm(key, w_parts, TN)
        bt_ref[h] = mm(u_rows, key, TN)
        lt_ref[h] = mm(go, query, TN) - mm(pulled, w_parts, TN)
        q_ref[h] = query
        u_ref[h] = u_rows
        w_ref[h] = w_rows
        pg_ref[h] = pulled
        col_ref[h, 0:count, 2:3] = query_scale


def scan_kernel(
    zn,
    a_ref,
    bt_ref,
    lt_ref,
    s0_ref,
    d0_ref,
    abuf,
    bbuf,
    lbuf,
    s_in,
    d_in,
    s_out,
    d_out,
    s_put,
    d_put,
    s_got,
    d_got,
    pre,
    xsend,
    xrecv,
    zsend,
    zrecv,
    psend,
    precv,
):
    seq, head = lax.axis_index("seq"), lax.axis_index("head")
    z, x = lax.div(seq, XN), lax.rem(seq, XN)
    heads, size = a_ref.shape[0], a_ref.shape[1]
    quarter = size // XN
    peers = [lax.rem(x + d, XN) for d in range(1, XN)]
    above = lax.rem(z + 1, zn)
    below = lax.rem(z + zn - 1, zn)

    def at(zz, xx):
        return (zz * XN + xx, head)

    barrier = pltpu.get_barrier_semaphore()
    for peer in peers:
        pl.semaphore_signal(barrier, inc=1, device_id=at(z, peer), device_id_type=MESH)
    for other in (above, below):
        pl.semaphore_signal(barrier, inc=1, device_id=at(other, x), device_id_type=MESH)
    pl.semaphore_wait(barrier, XN + 1)

    copies = []
    for i, peer in enumerate(peers):
        rows = pl.ds(pl.multiple_of(peer * quarter, quarter), quarter)
        for kind, (src, dst) in enumerate(
            ((a_ref, abuf.at[x]), (bt_ref.at[:, rows, :], bbuf.at[x]), (lt_ref.at[:, rows, :], lbuf.at[x]))
        ):
            copy = pltpu.make_async_remote_copy(
                src_ref=src,
                dst_ref=dst,
                send_sem=xsend.at[i, kind],
                recv_sem=xrecv.at[i, kind],
                device_id=at(z, peer),
                device_id_type=MESH,
            )
            copy.start()
            copies.append(copy)
    mine = pl.ds(pl.multiple_of(x * quarter, quarter), quarter)
    abuf[x] = a_ref[...]
    bbuf[x] = bt_ref[:, mine, :]
    lbuf[x] = lt_ref[:, mine, :]

    @pl.when(z == 0)
    def _():
        s_in[...] = jnp.zeros_like(s_in)

    @pl.when(z == zn - 1)
    def _():
        d_in[...] = jnp.zeros_like(d_in)

    for copy in copies:
        copy.wait()

    for h in range(heads):
        maps = [parts(abuf[j, h]) for j in range(XN)]
        p10 = mm(maps[1], maps[0])
        p32 = mm(maps[3], maps[2])
        p10s, p32s = parts(p10), parts(p32)
        p210 = mm(maps[2], p10s)
        p321 = mm(p32s, maps[1])
        total = mm(p32s, p10s)
        pre[h, 0] = abuf[0, h]
        pre[h, 1] = p10
        pre[h, 2] = p210
        pre[h, 3] = total
        pre[h, 4] = abuf[3, h]
        pre[h, 5] = p32
        pre[h, 6] = p321
        off = bbuf[0, h]
        s_put[1, h] = off
        for j in range(1, XN):
            off = mm(off, maps[j], NT) + bbuf[j, h]
            if j + 1 < XN:
                s_put[j + 1, h] = off
            else:
                s_out[h] = off
        off = lbuf[XN - 1, h]
        d_put[XN - 2, h] = off
        for j in range(XN - 2, -1, -1):
            off = mm(off, maps[j], NN) + lbuf[j, h]
            if j > 0:
                d_put[j - 1, h] = off
            else:
                d_out[h] = off

    s_hop = pltpu.make_async_remote_copy(
        src_ref=s_out, dst_ref=s_in, send_sem=zsend.at[0], recv_sem=zrecv.at[0], device_id=at(above, x), device_id_type=MESH
    )
    d_hop = pltpu.make_async_remote_copy(
        src_ref=d_out, dst_ref=d_in, send_sem=zsend.at[1], recv_sem=zrecv.at[1], device_id=at(below, x), device_id_type=MESH
    )

    def hand_out(put, got, kind):
        for i, peer in enumerate(peers):
            pltpu.make_async_remote_copy(
                src_ref=put.at[peer],
                dst_ref=got.at[x],
                send_sem=psend.at[i, kind],
                recv_sem=precv.at[i, kind],
                device_id=at(z, peer),
                device_id_type=MESH,
            ).start()
        got[x] = put[x]

    def forward():
        @pl.when(z > 0)
        def _():
            s_hop.wait_recv()

        @pl.when(z < zn - 1)
        def _():
            for h in range(heads):
                s_out[h] = s_out[h] + mm(s_in[h], pre[h, 3], NT)
            s_hop.start()

        for h in range(heads):
            state = s_in[h]
            pieces = parts(state)
            s_put[0, h] = state
            for j in range(1, XN):
                s_put[j, h] = s_put[j, h] + mm(pieces, pre[h, j - 1], NT)
        hand_out(s_put, s_got, 0)

    def backward():
        @pl.when(z < zn - 1)
        def _():
            d_hop.wait_recv()

        @pl.when(z > 0)
        def _():
            for h in range(heads):
                d_out[h] = d_out[h] + mm(d_in[h], pre[h, 3], NN)
            d_hop.start()

        for h in range(heads):
            state = d_in[h]
            pieces = parts(state)
            d_put[XN - 1, h] = state
            for j in range(XN - 1):
                d_put[j, h] = d_put[j, h] + mm(pieces, pre[h, 6 - j], NN)
        hand_out(d_put, d_got, 1)

    @pl.when(z < zn // 2)
    def _():
        forward()
        backward()

    @pl.when(z >= zn // 2)
    def _():
        backward()
        forward()

    @pl.when(z < zn - 1)
    def _():
        s_hop.wait_send()

    @pl.when(z > 0)
    def _():
        d_hop.wait_send()

    for kind, (put, got) in enumerate(((s_put, s_got), (d_put, d_got))):
        for i, peer in enumerate(peers):
            pltpu.make_async_remote_copy(
                src_ref=put.at[peer],
                dst_ref=got.at[x],
                send_sem=psend.at[i, kind],
                recv_sem=precv.at[i, kind],
                device_id=at(z, peer),
                device_id_type=MESH,
            ).wait()
    for j in range(XN):
        for h in range(heads):
            s0_ref[h, j * quarter : (j + 1) * quarter, :] = s_got[j, h]
            d0_ref[h, j * quarter : (j + 1) * quarter, :] = d_got[j, h]


def back_kernel(heads, q_ref, k_ref, v_ref, u_ref, w_ref, x_ref, pg_ref, col_ref, go_ref, s0_ref, d0_ref, gq_ref, gk_ref, gv_ref, gb_ref):
    size = HEAD_SIZE
    count = q_ref.shape[1]
    row, col, row_token, col_token, row_step, col_step = order_masks(count)
    strict = (col_token < row_token) | ((col_token == row_token) & row_step & ~col_step)
    smask = score_mask(count)
    for h in range(heads):
        query, key, value = q_ref[h], k_ref[h], v_ref[h]
        beta, key_scale = col_ref[h, :, 0:1], col_ref[h, :, 1:2]
        query_scale = col_ref[h, 0:count, 2:3]
        go = go_ref[:, h * size : (h + 1) * size]
        state, adjoint = parts(s0_ref[h]), parts(d0_ref[h])
        keys = parts(key)
        fresh = u_ref[h] - mm(w_ref[h], state, NT)
        rest = value - mm(keys, state, NT)
        d_fresh = pg_ref[h] + mm(keys, adjoint, NT)
        solved = mm(x_ref[h], d_fresh, TN)
        fresh_parts = parts(fresh)
        d_scores = parts(jnp.where(smask, mm(go, fresh_parts, NT), 0.0))
        d_system = jnp.where(strict, -mm(solved, fresh_parts, NT), 0.0)
        d_rest = beta * solved
        gram = mm(keys, keys, NT)
        d_beta = jnp.sum(solved * rest, axis=-1, keepdims=True) + jnp.sum(d_system * gram, axis=-1, keepdims=True)
        d_gram = parts(beta * d_system)
        d_query = mm(go, state) + mm(d_scores, keys)
        d_key = (
            mm(d_scores, query, TN)
            + mm(fresh_parts, adjoint)
            - mm(d_rest, state)
            + mm(d_gram, keys)
            + mm(d_gram, keys, TN)
        )
        d_query = query_scale * (d_query - query * jnp.sum(query * d_query, axis=-1, keepdims=True))
        d_key = key_scale * (d_key - key * jnp.sum(key * d_key, axis=-1, keepdims=True))
        d_logit = d_beta * beta * (1.0 - 0.5 * beta)
        gq_ref[:, h * size : (h + 1) * size] = d_query.astype(BF16)
        for j in range(NH):
            at = (h * NH + j) * size
            gk_ref[:, at : at + size] = d_key[j * count : (j + 1) * count].astype(BF16)
            gv_ref[:, at : at + size] = d_rest[j * count : (j + 1) * count].astype(BF16)
            gb_ref[:, h * NH + j : h * NH + j + 1] = d_logit[j * count : (j + 1) * count].astype(BF16)


def vmem(count):
    return [pl.BlockSpec(memory_space=pltpu.VMEM)] * count


def per_device(tokens, w_query, w_key, w_value, w_beta, grad_out):
    count = tokens.shape[0]
    size = HEAD_SIZE
    heads = w_query.shape[1] // size
    rows = NH * count
    quarter = size // XN
    zn = lax.axis_size("seq") // XN
    f32 = lambda *shape: jax.ShapeDtypeStruct(shape, F32)
    bf16 = lambda *shape: jax.ShapeDtypeStruct(shape, BF16)
    square = f32(heads, size, size)
    steps = f32(heads, rows, size)
    a, bt, lt, q, k, v, u, w, x, pg, cols = pl.pallas_call(
        functools.partial(front_kernel, heads),
        out_shape=(
            square,
            square,
            square,
            f32(heads, count, size),
            steps,
            steps,
            steps,
            steps,
            f32(heads, rows, rows),
            steps,
            f32(heads, rows, 8),
        ),
        in_specs=vmem(6),
        out_specs=tuple(vmem(11)),
        name="front",
    )(tokens, w_query, w_key, w_value, w_beta, grad_out)
    s0, d0 = pl.pallas_call(
        functools.partial(scan_kernel, zn),
        out_shape=(square, square),
        in_specs=vmem(3),
        out_specs=tuple(vmem(2)),
        scratch_shapes=[
            pltpu.VMEM((XN, heads, size, size), F32),
            pltpu.VMEM((XN, heads, quarter, size), F32),
            pltpu.VMEM((XN, heads, quarter, size), F32),
            pltpu.VMEM((heads, quarter, size), F32),
            pltpu.VMEM((heads, quarter, size), F32),
            pltpu.VMEM((heads, quarter, size), F32),
            pltpu.VMEM((heads, quarter, size), F32),
            pltpu.VMEM((XN, heads, quarter, size), F32),
            pltpu.VMEM((XN, heads, quarter, size), F32),
            pltpu.VMEM((XN, heads, quarter, size), F32),
            pltpu.VMEM((XN, heads, quarter, size), F32),
            pltpu.VMEM((heads, 7, size, size), F32),
            pltpu.SemaphoreType.DMA((XN - 1, 3)),
            pltpu.SemaphoreType.DMA((XN - 1, 3)),
            pltpu.SemaphoreType.DMA((2,)),
            pltpu.SemaphoreType.DMA((2,)),
            pltpu.SemaphoreType.DMA((XN - 1, 2)),
            pltpu.SemaphoreType.DMA((XN - 1, 2)),
        ],
        compiler_params=pltpu.CompilerParams(collective_id=0, has_side_effects=True),
        name="scan",
    )(a, bt, lt)
    gq, gk, gv, gb = pl.pallas_call(
        functools.partial(back_kernel, heads),
        out_shape=(
            bf16(count, heads * size),
            bf16(count, heads * NH * size),
            bf16(count, heads * NH * size),
            bf16(count, heads * NH),
        ),
        in_specs=vmem(11),
        out_specs=tuple(vmem(4)),
        name="back",
    )(q, k, v, u, w, x, pg, cols, grad_out, s0, d0)

    rounded = (gq, gk, gv, gb)
    weights = (w_query, w_key, w_value, w_beta)
    grad_all = jnp.concatenate(rounded, axis=1)
    summed = lax.psum_scatter(
        lax.dot_general(tokens, grad_all, (((0,), (0,)), ((), ())), preferred_element_type=F32).astype(BF16),
        "seq",
        scatter_dimension=0,
        tiled=True,
    ).astype(F32)
    first = gq.shape[1]
    second = first + gk.shape[1]
    third = second + gv.shape[1]
    input_term = sum(dg(g, wt, NT) for g, wt in zip(rounded, weights))
    grad_tokens = lax.psum_scatter(input_term.astype(BF16), "head", scatter_dimension=1, tiled=True)
    return (grad_tokens, summed[:, :first], summed[:, first:second], summed[:, second:third], summed[:, third:])


def solution(mesh):
    in_specs = (
        P("seq", None),
        P(None, "head"),
        P(None, "head"),
        P(None, "head"),
        P(None, "head"),
        P("seq", "head"),
    )
    return jax.shard_map(
        per_device, mesh=mesh, in_specs=in_specs, out_specs=(P("seq", "head"),) * 5, check_vma=False
    )
```

time: 1260 us -> 354 us (0.28)
  waiting for transfers between devices: 747 us -> 254 us
  other arithmetic: 176 us -> 0 us
  starting transfers between devices: 152 us -> 0.08 us
  matrix products: 119 us -> 8.1 us
  Pallas kernels: 0 us -> 60.6 us
  local copies, waits for them, and re-layouts: 49.4 us -> 16.2 us
    ppermute x62 -> x0, waiting for transfers between devices: 450 us -> none  [passed_along(): return lax.ppermute(array, axis, pairs)]
    another operation x28 -> x0, other arithmetic: 164 us -> none  [block_weights(): lax.linalg.triangular_solve(system, jnp.diag(beta_rows), left_side=True,...]
    ppermute x62 -> x0, starting transfers between devices: 152 us -> none  [passed_along(): return lax.ppermute(array, axis, pairs)]
    dot_general x144 -> x4, matrix products: 105 us -> 3.17 us  [dg(): lax.dot_general(left, right, (dims, ((), ())), preferred_element_type=F32)]
    pallas_call x0 -> x3, Pallas kernels: none -> 60.6 us  [the longest x1 44.6 us: per_device(): pl.pallas_call(functools.partial(scan_kernel, zn), out_shape=(square, squ...]
    unnamed x3, waiting for transfers between devices: 265 us -> 222 us
  transfers between devices with their start and end apart: 64 -> 2, of which waited for: 64 -> 2; matrix products, arithmetic and copies ran while one was open for 1% -> 2% of each run, Pallas kernels for 0% -> 0%
where the time goes in v1:
time: 354 us; the launch traced here: 353 us
  waiting for transfers between devices  254 us (72%)
  Pallas kernels  60.6 us (17%)
  local copies, waits for them, and re-layouts  16.2 us (5%)
  between operations  14.1 us (4%)
  matrix products  8.1 us (2%)
    unnamed x3, waiting for transfers between devices  222 us
    pallas_call x1, Pallas kernels, per_device(): pl.pallas_call(functools.partial(scan_kernel, zn), out_shape=(square, squ...  44.6 us
    reduce_scatter x1, waiting for transfers between devices, per_device(): lax.psum_scatter(input_term.astype(BF16), 'head', scatter_dimension=1, ti...  31.9 us
    unnamed x24, local copies, waits for them, and re-layouts  15.5 us
    pallas_call x1, Pallas kernels, per_device(): pl.pallas_call(functools.partial(front_kernel, heads), out_shape=(square,...  11 us
  transfers between devices with their start and end apart: 2, of which 2 were waited for; matrix products, arithmetic and copies ran while one was open for 2% of the time, Pallas kernels for 0%

profile of v1, /device:TPU:32, one launch (start us, length us, event | category | flops | bytes accessed | tf_op | source)
XLA Modules:
  0.0 352.7 jit_solution(10651061209818991891)
XLA Ops:
  7.2 0.0 reduce-scatter.7.cloned.1.call-start
  7.2 1.8 copy.15.wb_ref
  9.0 11.0 %front.1 = (f32[2,128,128]{2,1,0:T(8,128)}, f32[2,128,128]{2,1,0:T(8,128)}, f32[2,128,128]{2,1,0:T(8,128)}, f32[2,128,128]{2,1,0:T(8,128)}, f32[2,256,128]{2,1,0...) custom-call(bf16[128,2048]{1,0:T(8,128)(2,1)} %tokens_ref.1, ...), custom_call_target="tpu_custom_call" | custom-call | tf_op jit(solution)/shard_map/front/pallas_call | solution.py:408
  20.0 44.6 %scan.1 = (f32[2,128,128]{2,1,0:T(8,128)}, f32[2,128,128]{2,1,0:T(8,128)}) custom-call(f32[2,128,128]{2,1,0:T(8,128)} %get-tuple-element.30.a_ref, f32[2,128,128]{2,1,0:T(8,128)} %get-tuple-element.31.bt_ref, f32[2,128,128]{2,1,0:T(8,128)} %get-tuple-element.32.lt_ref), custom_call_target="tpu_custom_call" | custom-call | tf_op jit(solution)/shard_map/scan/pallas_call | solution.py:427
  64.5 5.0 %back.1 = (bf16[128,256]{1,0:T(8,128)(2,1)}, bf16[128,512]{1,0:T(8,128)(2,1)}, bf16[128,512]{1,0:T(8,128)(2,1)}, bf16[128,4]{1,0:T(8,128)(2,1)}) custom-call(f32[2,128,128]{2,1,0:T(8,128)} %get-tuple-element.22.q_ref, f32[2,256,128]{2,1,0:T(8,128)} %get-tuple-element.23.k_ref, f32[2,256,128]{2,1,0:T(8,128)} %get-tuple-element.24.v_ref, ...), custom_call_target="tpu_custom_call" | custom-call | tf_op jit(solution)/shard_map/back/pallas_call | solution.py:455
  69.6 4.9 %fusion = bf16[2048,1284]{0,1:T(8,128)(2,1)} fusion(bf16[128,2048]{1,0:T(8,128)(2,1)S(1)} %copy-done.3, bf16[128,4]{1,0:T(8,128)(2,1)} %get-tuple-element.38, bf16[128,512]{1,0:T(8,128)(2,1)} %get-tuple-element.37, bf16[128,512]{1,0:T(8,128)(2,1)} %get-tuple-element.36, bf16[128,256]{1,0:T(8,128)(2,1)} %get-tuple-element.35), kind=kOutput, calls=%fused_computation.1 | convolution fusion | flops 677130240 | bytes 6112256 | tf_op jit(solution)/shard_map/dot_general | solution.py:472
  74.5 8.2 %copy.19 = bf16[2048,1284]{1,0:T(8,128)(2,1)} copy(bf16[2048,1284]{0,1:T(8,128)(2,1)} %fusion) | data formatting | bytes 10518528
  82.7 0.0 reduce-scatter.7.cloned.1.call-update
  82.7 0.0 reduce-scatter.5.cloned.1.call-start
  82.8 1.1 copy-done.2
  83.9 0.5 fusion.11
  84.4 0.3 copy-done
  84.7 0.8 convolution_add_fusion.2
  85.5 0.8 copy-done.1
  86.3 0.8 convolution_add_fusion.1
  87.1 1.1 fusion.1
  88.2 0.0 reduce-scatter.5.cloned.1.call-update
  88.2 221.7 %reduce-scatter.7.cloned.1.call-done = bf16[64,1284]{1,0:T(8,128)(2,1)} async-done(((bf16[2048,1284]{1,0:T(8,128)(2,1)}), bf16[64,1284]{1,0:T(8,128)(2,1)}) %reduce-scatter.7.cloned.1.call-update) | async-done | bytes 164368
  309.9 1.1 copy.20
  311.0 0.6 slice.19
  311.6 0.7 copy.16
  312.4 0.8 copy.18
  313.2 0.8 copy.17
  313.9 31.9 %reduce-scatter.5.cloned.1.call-done = bf16[128,256]{1,0:T(8,128)(2,1)} async-done(((bf16[128,2048]{1,0:T(8,128)(2,1)}), bf16[128,256]{1,0:T(8,128)(2,1)}) %reduce-scatter.5.cloned.1.call-update) | async-done | bytes 65552 | tf_op jit(solution)/shard_map/reduce_scatter | solution.py:481
  (17 shorter events, 0.1 us)
Async XLA Ops:
  7.2 302.7 %reduce-scatter.7.cloned.1.call-start = ((), (), s32[]{:S(2)}) async-start(), calls=%async_computation.3 | async-start | bytes 5947392
  20.0 49.6 %copy-start.3 = (bf16[128,2048]{1,0:T(8,128)(2,1)S(1)}, bf16[128,2048]{1,0:T(8,128)(2,1)}, u32[]{:S(2)}) copy-start(bf16[128,2048]{1,0:T(8,128)(2,1)} %tokens_ref.1) | copy-start | bytes 1572868
  82.7 1.2 copy-start.2
  82.7 1.2 copy-start.6
  82.7 1.7 copy-start.5
  82.7 2.0 copy-start
  82.7 263.2 %reduce-scatter.5.cloned.1.call-start = ((), (), s32[]{:S(2)}) async-start(), calls=%async_computation.2 | async-start | bytes 589824 | tf_op jit(solution)/shard_map/reduce_scatter | solution.py:481
  84.7 1.6 copy-start.1
  84.7 1.6 copy-start.4
  86.3 0.8 copy-start.7
  86.3 0.8 copy-start.8
Sparse Core Ops, SparseCore 0:
  82.8 227.0 reduce-scatter.6
  313.0 32.8 reduce-scatter.4

commit v2 on v1

--- a/solution.py
+++ b/solution.py
@@ -89,7 +89,7 @@
     pq = dg(tok, wq_ref[...], NN)
     pk = dg(tok, wk_ref[...], NN)
     pv = dg(tok, wv_ref[...], NN)
-    pb = dg(tok, wb_ref[...], NN)
+    pb = dg(tok, wb_ref[...], NT)
     beta_all = 2.0 * jax.nn.sigmoid(pb)
     row, col, row_token, col_token, row_step, col_step = order_masks(count)
     strict = (col_token < row_token) | ((col_token == row_token) & row_step & ~col_step)
@@ -153,8 +153,10 @@
     a_ref,
     bt_ref,
     lt_ref,
+    tok_ref,
     s0_ref,
     d0_ref,
+    tt_ref,
     abuf,
     bbuf,
     lbuf,
@@ -173,6 +175,10 @@
     zrecv,
     psend,
     precv,
+    tokt,
+    ttbuf,
+    tsend,
+    trecv,
 ):
     seq, head = lax.axis_index("seq"), lax.axis_index("head")
     z, x = lax.div(seq, XN), lax.rem(seq, XN)
@@ -221,8 +227,29 @@
     def _():
         d_in[...] = jnp.zeros_like(d_in)
 
+    rows = tok_ref.shape[1] // (zn * XN)
+    for zz in range(zn):
+        block = tok_ref[:, zz * XN * rows : (zz + 1) * XN * rows]
+        tokt[zz] = block.T.reshape(XN, rows, block.shape[0])
+
     for copy in copies:
         copy.wait()
+
+    count = tok_ref.shape[0]
+    lanes = pl.ds(pl.multiple_of(x * count, count), count)
+    t_copies = []
+    for i, peer in enumerate(peers):
+        copy = pltpu.make_async_remote_copy(
+            src_ref=tokt.at[:, peer],
+            dst_ref=ttbuf.at[:, :, lanes],
+            send_sem=tsend.at[i],
+            recv_sem=trecv.at[i],
+            device_id=at(z, peer),
+            device_id_type=MESH,
+        )
+        copy.start()
+        t_copies.append(copy)
+    ttbuf[:, :, lanes] = tokt[:, x]
 
     for h in range(heads):
         maps = [parts(abuf[j, h]) for j in range(XN)]
@@ -341,18 +368,22 @@
                 device_id=at(z, peer),
                 device_id_type=MESH,
             ).wait()
+    for copy in t_copies:
+        copy.wait()
+    tt_ref[...] = ttbuf[...]
     for j in range(XN):
         for h in range(heads):
             s0_ref[h, j * quarter : (j + 1) * quarter, :] = s_got[j, h]
             d0_ref[h, j * quarter : (j + 1) * quarter, :] = d_got[j, h]
 
 
-def back_kernel(heads, q_ref, k_ref, v_ref, u_ref, w_ref, x_ref, pg_ref, col_ref, go_ref, s0_ref, d0_ref, gq_ref, gk_ref, gv_ref, gb_ref):
+def back_kernel(heads, q_ref, k_ref, v_ref, u_ref, w_ref, x_ref, pg_ref, col_ref, go_ref, s0_ref, d0_ref, g_ref):
     size = HEAD_SIZE
     count = q_ref.shape[1]
     row, col, row_token, col_token, row_step, col_step = order_masks(count)
     strict = (col_token < row_token) | ((col_token == row_token) & row_step & ~col_step)
     smask = score_mask(count)
+    logits = []
     for h in range(heads):
         query, key, value = q_ref[h], k_ref[h], v_ref[h]
         beta, key_scale = col_ref[h, :, 0:1], col_ref[h, :, 1:2]
@@ -382,12 +413,244 @@
         d_query = query_scale * (d_query - query * jnp.sum(query * d_query, axis=-1, keepdims=True))
         d_key = key_scale * (d_key - key * jnp.sum(key * d_key, axis=-1, keepdims=True))
         d_logit = d_beta * beta * (1.0 - 0.5 * beta)
-        gq_ref[:, h * size : (h + 1) * size] = d_query.astype(BF16)
+        g_ref[:, h * size : (h + 1) * size] = d_query.astype(BF16)
         for j in range(NH):
-            at = (h * NH + j) * size
-            gk_ref[:, at : at + size] = d_key[j * count : (j + 1) * count].astype(BF16)
-            gv_ref[:, at : at + size] = d_rest[j * count : (j + 1) * count].astype(BF16)
-            gb_ref[:, h * NH + j : h * NH + j + 1] = d_logit[j * count : (j + 1) * count].astype(BF16)
+            at = (heads + h * NH + j) * size
+            g_ref[:, at : at + size] = d_key[j * count : (j + 1) * count].astype(BF16)
+            at += heads * NH * size
+            g_ref[:, at : at + size] = d_rest[j * count : (j + 1) * count].astype(BF16)
+            logits.append(d_logit[j * count : (j + 1) * count])
+    pad = jnp.zeros((count, size - len(logits)), F32)
+    g_ref[:, heads * (1 + 2 * NH) * size :] = jnp.concatenate(logits + [pad], axis=1).astype(BF16)
+
+
+def tail_kernel(
+    zn,
+    yn,
+    g_ref,
+    tt_ref,
+    wq_hbm,
+    wk_hbm,
+    wv_hbm,
+    wb_hbm,
+    gx_ref,
+    gwq_ref,
+    gwk_ref,
+    gwv_ref,
+    gwb_ref,
+    wq,
+    wk,
+    wv,
+    wb,
+    gbuf,
+    part,
+    ring_a,
+    ring_b,
+    got_a,
+    got_b,
+    pair_put,
+    pair_got,
+    y_put,
+    y_got,
+    wsem,
+    gsend,
+    grecv,
+    rsend,
+    rrecv,
+    csend,
+    crecv,
+    ysend,
+    yrecv,
+):
+    seq, head = lax.axis_index("seq"), lax.axis_index("head")
+    z, x = lax.div(seq, XN), lax.rem(seq, XN)
+    y, core = lax.div(head, 2), lax.rem(head, 2)
+    above, below = lax.rem(z + 1, zn), lax.rem(z + zn - 1, zn)
+    right, left = lax.rem(x + 1, XN), lax.rem(x + XN - 1, XN)
+    partner = head + 1 - 2 * core
+    count, width = g_ref.shape
+    q_wide, k_wide, v_wide = wq.shape[1], wk.shape[1], wv.shape[1]
+    beta_at = q_wide + k_wide + v_wide
+    betas = wb.shape[0]
+    rows = part.shape[1]
+    block = gx_ref.shape[1]
+
+    loads = [
+        pltpu.make_async_copy(src, dst, wsem.at[i])
+        for i, (src, dst) in enumerate(((wq_hbm, wq), (wk_hbm, wk), (wv_hbm, wv), (wb_hbm, wb)))
+    ]
+    for load in loads:
+        load.start()
+
+    barrier = pltpu.get_barrier_semaphore()
+    greeted = [(z * XN + right, head), (z * XN + left, head), (above * XN + x, head), (below * XN + x, head), (seq, partner)]
+    greeted += [(seq, lax.rem(y + d, yn) * 2 + core) for d in range(1, yn)]
+    for device in greeted:
+        pl.semaphore_signal(barrier, inc=1, device_id=device, device_id_type=MESH)
+    pl.semaphore_wait(barrier, len(greeted))
+
+    half = q_wide + k_wide
+    mid_a, mid_b = half // 2, half + 3 * 128
+    pieces = ((0, mid_a, 0, 0), (half, mid_b, 1, 0), (mid_a, half, 0, mid_a), (mid_b, width, 1, mid_b - half))
+
+    def block_rows(member):
+        return pl.ds(pl.multiple_of(member * count, count), count)
+
+    def own_copy(p, way):
+        lo, hi = pieces[p][:2]
+        return pltpu.make_async_remote_copy(
+            src_ref=g_ref.at[:, lo:hi],
+            dst_ref=gbuf.at[block_rows(x), lo:hi],
+            send_sem=gsend.at[p, way],
+            recv_sem=grecv.at[p, way],
+            device_id=(z * XN + (right if way == 0 else left), head),
+            device_id_type=MESH,
+        )
+
+    def onward_copy(p):
+        lo, hi = pieces[p][:2]
+        to_right = p < 2
+        spot = gbuf.at[block_rows(left if to_right else right), lo:hi]
+        return pltpu.make_async_remote_copy(
+            src_ref=spot,
+            dst_ref=spot,
+            send_sem=gsend.at[p, 2],
+            recv_sem=grecv.at[p, 2],
+            device_id=(z * XN + (right if to_right else left), head),
+            device_id_type=MESH,
+        )
+
+    def offer(p):
+        own_copy(p, 0).start()
+        own_copy(p, 1).start()
+
+    def relay(p):
+        own_copy(p, 0).wait_recv()
+        own_copy(p, 1).wait_recv()
+        onward_copy(p).start()
+
+    offer(0)
+    offer(1)
+    gbuf[block_rows(x), :] = g_ref[...]
+    for load in loads:
+        load.wait()
+
+    def input_term(d, side):
+        lo = pl.multiple_of((lax.rem(y + d, yn) * 2 + side) * block, block)
+        spot = pl.ds(lo, block)
+        total = dg(g_ref[:, :q_wide], wq[spot, :], NT)
+        total = total + dg(g_ref[:, q_wide:half], wk[spot, :], NT)
+        total = total + dg(g_ref[:, half:beta_at], wv[spot, :], NT)
+        return total + dg(g_ref[:, beta_at : beta_at + betas], wb[:, spot], NN)
+
+    def pair_copy(d):
+        return pltpu.make_async_remote_copy(
+            src_ref=pair_put.at[d],
+            dst_ref=pair_got.at[d],
+            send_sem=csend.at[d],
+            recv_sem=crecv.at[d],
+            device_id=(seq, partner),
+            device_id_type=MESH,
+        )
+
+    def y_copy(d):
+        return pltpu.make_async_remote_copy(
+            src_ref=y_put.at[d - 1],
+            dst_ref=y_got.at[d - 1],
+            send_sem=ysend.at[d - 1],
+            recv_sem=yrecv.at[d - 1],
+            device_id=(seq, lax.rem(y + d, yn) * 2 + core),
+            device_id_type=MESH,
+        )
+
+    order = list(range(1, yn)) + [0]
+    for d in order:
+        pair_put[d] = input_term(d, 1 - core).astype(BF16)
+        pair_copy(d).start()
+    relay(0)
+    offer(2)
+    relay(1)
+    offer(3)
+    kept = None
+    for d in order:
+        term = input_term(d, core)
+        pair_copy(d).wait_recv()
+        term = term + pair_got[d].astype(F32)
+        if d:
+            y_put[d - 1] = term.astype(BF16)
+            y_copy(d).start()
+        else:
+            gx_ref[...] = term
+
+    rings = ((ring_a, got_a), (ring_b, got_b))
+
+    def hop(p, step):
+        lo, hi, way, at = pieces[p]
+        put, got = rings[way]
+        return pltpu.make_async_remote_copy(
+            src_ref=put.at[step, :, at : at + hi - lo],
+            dst_ref=got.at[step, :, at : at + hi - lo],
+            send_sem=rsend.at[p, step],
+            recv_sem=rrecv.at[p, step],
+            device_id=((below if way else above) * XN + x, head),
+            device_id_type=MESH,
+        )
+
+    def store(lo, value):
+        for i in range(value.shape[1] // 128):
+            at = lo + i * 128
+            piece = value[:, i * 128 : (i + 1) * 128]
+            if at < q_wide:
+                gwq_ref[:, at : at + 128] = piece
+            elif at < half:
+                gwk_ref[:, at - q_wide : at - q_wide + 128] = piece
+            elif at < beta_at:
+                gwv_ref[:, at - half : at - half + 128] = piece
+            else:
+                gwb_ref[...] = piece[:, :betas]
+
+    def ring_step(p, step):
+        lo, hi, way, at = pieces[p]
+        put, got = rings[way]
+        if step == 0:
+            onward_copy(p).wait_recv()
+            part[:, :, lo:hi] = dg(tt_ref[...].reshape(zn * rows, XN * count), gbuf[:, lo:hi], NN).reshape(zn, rows, hi - lo)
+        chunk = lax.rem(z + 1 + step, zn) if way else lax.rem(z + 2 * zn - 1 - step, zn)
+        value = part[chunk, :, lo:hi]
+        if step > 0:
+            hop(p, step - 1).wait_recv()
+            value = value + got[step - 1, :, at : at + hi - lo].astype(F32)
+        if step < zn - 1:
+            put[step, :, at : at + hi - lo] = value.astype(BF16)
+            hop(p, step).start()
+        else:
+            store(lo, value)
+
+    delay = (0, 0, 1, 1)
+    for turn in range(zn + max(delay)):
+        for p in range(len(pieces)):
+            step = turn - delay[p]
+            if step == 0 and p >= 2:
+                relay(p)
+            if 0 <= step < zn:
+                ring_step(p, step)
+
+    total = gx_ref[...]
+    for d in range(1, yn):
+        y_copy(d).wait_recv()
+        total = total + y_got[d - 1].astype(F32)
+    gx_ref[...] = total
+
+    for p in range(len(pieces)):
+        own_copy(p, 0).wait_send()
+        own_copy(p, 1).wait_send()
+        onward_copy(p).wait_send()
+        for step in range(zn - 1):
+            hop(p, step).wait_send()
+    for d in range(yn):
+        pair_copy(d).wait_send()
+        if d:
+            y_copy(d).wait_send()
 
 
 def vmem(count):
@@ -400,6 +663,8 @@
     heads = w_query.shape[1] // size
     rows = NH * count
     quarter = size // XN
+    w_beta_t = w_beta.T
+    shard = tokens.shape[1] // lax.axis_size("seq")
     zn = lax.axis_size("seq") // XN
     f32 = lambda *shape: jax.ShapeDtypeStruct(shape, F32)
     bf16 = lambda *shape: jax.ShapeDtypeStruct(shape, BF16)
@@ -423,12 +688,12 @@
         in_specs=vmem(6),
         out_specs=tuple(vmem(11)),
         name="front",
-    )(tokens, w_query, w_key, w_value, w_beta, grad_out)
-    s0, d0 = pl.pallas_call(
+    )(tokens, w_query, w_key, w_value, w_beta_t, grad_out)
+    s0, d0, tt = pl.pallas_call(
         functools.partial(scan_kernel, zn),
-        out_shape=(square, square),
-        in_specs=vmem(3),
-        out_specs=tuple(vmem(2)),
+        out_shape=(square, square, bf16(zn, shard, XN * count)),
+        in_specs=vmem(4),
+        out_specs=tuple(vmem(3)),
         scratch_shapes=[
             pltpu.VMEM((XN, heads, size, size), F32),
             pltpu.VMEM((XN, heads, quarter, size), F32),
@@ -448,38 +713,67 @@
             pltpu.SemaphoreType.DMA((2,)),
             pltpu.SemaphoreType.DMA((XN - 1, 2)),
             pltpu.SemaphoreType.DMA((XN - 1, 2)),
+            pltpu.VMEM((zn, XN, shard, count), BF16),
+            pltpu.VMEM((zn, shard, XN * count), BF16),
+            pltpu.SemaphoreType.DMA((XN - 1,)),
+            pltpu.SemaphoreType.DMA((XN - 1,)),
         ],
         compiler_params=pltpu.CompilerParams(collective_id=0, has_side_effects=True),
         name="scan",
-    )(a, bt, lt)
-    gq, gk, gv, gb = pl.pallas_call(
+    )(a, bt, lt, tokens)
+    width = heads * (1 + 2 * NH) * size + 128
+    grads = pl.pallas_call(
         functools.partial(back_kernel, heads),
-        out_shape=(
-            bf16(count, heads * size),
-            bf16(count, heads * NH * size),
-            bf16(count, heads * NH * size),
-            bf16(count, heads * NH),
-        ),
+        out_shape=bf16(count, width),
         in_specs=vmem(11),
-        out_specs=tuple(vmem(4)),
+        out_specs=pl.BlockSpec(memory_space=pltpu.VMEM),
         name="back",
     )(q, k, v, u, w, x, pg, cols, grad_out, s0, d0)
 
-    rounded = (gq, gk, gv, gb)
-    weights = (w_query, w_key, w_value, w_beta)
-    grad_all = jnp.concatenate(rounded, axis=1)
-    summed = lax.psum_scatter(
-        lax.dot_general(tokens, grad_all, (((0,), (0,)), ((), ())), preferred_element_type=F32).astype(BF16),
-        "seq",
-        scatter_dimension=0,
-        tiled=True,
-    ).astype(F32)
-    first = gq.shape[1]
-    second = first + gk.shape[1]
-    third = second + gv.shape[1]
-    input_term = sum(dg(g, wt, NT) for g, wt in zip(rounded, weights))
-    grad_tokens = lax.psum_scatter(input_term.astype(BF16), "head", scatter_dimension=1, tiled=True)
-    return (grad_tokens, summed[:, :first], summed[:, first:second], summed[:, second:third], summed[:, third:])
+    yn = lax.axis_size("head") // 2
+    block = tokens.shape[1] // (2 * yn)
+    half = heads * (1 + NH) * size
+    dma = pltpu.SemaphoreType.DMA
+    gx, gwq, gwk, gwv, gwb = pl.pallas_call(
+        functools.partial(tail_kernel, zn, yn),
+        out_shape=(
+            f32(count, block),
+            f32(shard, w_query.shape[1]),
+            f32(shard, w_key.shape[1]),
+            f32(shard, w_value.shape[1]),
+            f32(shard, w_beta.shape[1]),
+        ),
+        in_specs=vmem(2) + [pl.BlockSpec(memory_space=pl.ANY)] * 4,
+        out_specs=tuple(vmem(5)),
+        scratch_shapes=[
+            pltpu.VMEM(w_query.shape, BF16),
+            pltpu.VMEM(w_key.shape, BF16),
+            pltpu.VMEM(w_value.shape, BF16),
+            pltpu.VMEM(w_beta_t.shape, BF16),
+            pltpu.VMEM((XN * count, width), BF16),
+            pltpu.VMEM((zn, shard, width), F32),
+            pltpu.VMEM((zn - 1, shard, half), BF16),
+            pltpu.VMEM((zn - 1, shard, width - half), BF16),
+            pltpu.VMEM((zn - 1, shard, half), BF16),
+            pltpu.VMEM((zn - 1, shard, width - half), BF16),
+            pltpu.VMEM((yn, count, block), BF16),
+            pltpu.VMEM((yn, count, block), BF16),
+            pltpu.VMEM((yn - 1, count, block), BF16),
+            pltpu.VMEM((yn - 1, count, block), BF16),
+            dma((4,)),
+            dma((4, 3)),
+            dma((4, 3)),
+            dma((4, zn - 1)),
+            dma((4, zn - 1)),
+            dma((yn,)),
+            dma((yn,)),
+            dma((yn - 1,)),
+            dma((yn - 1,)),
+        ],
+        compiler_params=pltpu.CompilerParams(collective_id=1, has_side_effects=True),
+        name="tail",
+    )(grads, tt, w_query, w_key, w_value, w_beta_t)
+    return (gx.astype(BF16), gwq, gwk, gwv, gwb)
 
 
 def solution(mesh):

time: 354 us -> 124 us (0.35)
  waiting for transfers between devices: 254 us -> 0 us
  Pallas kernels: 60.6 us -> 114 us
  between operations: 14.1 us -> 0.65 us
  local copies, waits for them, and re-layouts: 16.2 us -> 6.01 us
  matrix products: 8.1 us -> 0 us
    unnamed x3 -> x0, waiting for transfers between devices: 222 us -> none
    pallas_call x1 -> x2, Pallas kernels: 5.04 us -> 58 us  [the longest x1 53 us: per_device(): pl.pallas_call(functools.partial(tail_kernel, zn, yn), out_shape=(f32(cou...]
    reduce_scatter x1 -> x0, waiting for transfers between devices: 31.9 us -> none  [per_device(): lax.psum_scatter(input_term.astype(BF16), 'head', scatter_dimension=1, ti...]
    unnamed x24 -> x4, local copies, waits for them, and re-layouts: 15.5 us -> 6.01 us
    dot_general x5 -> x0, matrix products: 8.1 us -> none  [the longest x1 4.93 us: per_device(): lax.dot_general(tokens, grad_all, (((0,), (0,)), ((), ())), preferred_ele...]
  transfers between devices with their start and end apart: 2 -> 0, of which waited for: 2 -> 0; matrix products, arithmetic and copies ran while one was open for 2% -> 0% of each run, Pallas kernels for 0% -> 0%
where the time goes in v2:
time: 124 us; the launch traced here: 122 us
  Pallas kernels  114 us (92%)
  local copies, waits for them, and re-layouts  6.01 us (5%)
  other arithmetic  1.54 us (1%)
    pallas_call x1, Pallas kernels, per_device(): pl.pallas_call(functools.partial(tail_kernel, zn, yn), out_shape=(f32(cou...  53 us
    pallas_call x1, Pallas kernels, per_device(): pl.pallas_call(functools.partial(scan_kernel, zn), out_shape=(square, squ...  45 us
    pallas_call x1, Pallas kernels, per_device(): pl.pallas_call(functools.partial(front_kernel, heads), out_shape=(square,...  10.9 us
    unnamed x4, local copies, waits for them, and re-layouts  6.01 us
    pallas_call x1, Pallas kernels, per_device(): pl.pallas_call(functools.partial(back_kernel, heads), out_shape=bf16(coun...  5.03 us

profile of v2, /device:TPU:32, one launch (start us, length us, event | category | flops | bytes accessed | tf_op | source)
XLA Modules:
  0.0 122.1 jit_solution(3986815388520042248)
XLA Ops:
  0.6 10.9 %front.1 = (f32[2,128,128]{2,1,0:T(8,128)}, f32[2,128,128]{2,1,0:T(8,128)}, f32[2,128,128]{2,1,0:T(8,128)}, f32[2,128,128]{2,1,0:T(8,128)}, f32[2,256,128]{2,1,0...) custom-call(bf16[128,2048]{1,0:T(8,128)(2,1)} %tok_ref.1, ...), custom_call_target="tpu_custom_call" | custom-call | tf_op jit(solution)/shard_map/front/pallas_call | solution.py:673
  11.5 45.0 %scan.1 = (f32[2,128,128]{2,1,0:T(8,128)}, f32[2,128,128]{2,1,0:T(8,128)}, bf16[8,64,512]{2,1,0:T(8,128)(2,1)}) custom-call(f32[2,128,128]{2,1,0:T(8,128)} %get-tuple-element.32.a_ref, f32[2,128,128]{2,1,0:T(8,128)} %get-tuple-element.33.bt_ref, f32[2,128,128]{2,1,0:T(8,128)} %get-tuple-element.34.lt_ref, bf16[128,2048]{1,0:T(8,128)(2,1)} %tok_ref.1), custom_call_target="tpu_custom_call" | custom-call | tf_op jit(solution)/shard_map/scan/pallas_call | solution.py:692
  56.5 5.0 %back.1.g_ref = bf16[128,1408]{1,0:T(8,128)(2,1)} custom-call(f32[2,128,128]{2,1,0:T(8,128)} %get-tuple-element.24.q_ref, f32[2,256,128]{2,1,0:T(8,128)} %get-tuple-element.25.k_ref, f32[2,256,128]{2,1,0:T(8,128)} %get-tuple-element.26.v_ref, f32[2,256,128]{2,1,0:T(8,128)} %get-tuple-element.27.u_ref, f32[2,256,128]{2,1,0:T(8,128)} %get-tuple-element.28.w_ref, ...), custom_call_target="tpu_custom_call" | custom-call | tf_op jit(solution)/shard_map/back/pallas_call | solution.py:725
  61.6 53.0 %tail.1 = (f32[128,256]{1,0:T(8,128)}, f32[64,256]{1,0:T(8,128)}, f32[64,512]{1,0:T(8,128)}, f32[64,512]{1,0:T(8,128)}, f32[64,4]{1,0:T(8,128)}) custom-call(bf16[128,1408]{1,0:T(8,128)(2,1)} %back.1.g_ref, bf16[8,64,512]{2,1,0:T(8,128)(2,1)} %get-tuple-element.37.tt_ref, bf16[2048,256]{1,0:T(8,128)(2,1)} %wq_hbm.1, bf16[2048,512]{1,0:T(8,128)(2,1)} %wk_hbm.1, ...), custom_call_target="tpu_custom_call" | custom-call | tf_op jit(solution)/shard_map/tail/pallas_call | solution.py:737
  114.6 1.5 %convert_element_type.3 = bf16[128,256]{1,0:T(8,128)(2,1)} convert(f32[128,256]{1,0:T(8,128)} %get-tuple-element.38) | non-fusion elementwise | flops 32768 | bytes 196608 | tf_op jit(solution)/shard_map/convert_element_type | solution.py:776
  116.1 1.4 %copy.11 = f32[64,4]{0,1:T(4,128)} copy(f32[64,4]{1,0:T(8,128)} %get-tuple-element.47) | data formatting | bytes 2048
  117.5 1.5 %copy.15 = f32[64,256]{1,0:T(8,128)} copy(f32[64,256]{1,0:T(8,128)} %get-tuple-element.54) | data formatting | bytes 131072
  119.0 1.6 %copy.16 = f32[64,512]{1,0:T(8,128)} copy(f32[64,512]{1,0:T(8,128)} %get-tuple-element.55) | data formatting | bytes 262144
  120.6 1.6 %copy.17 = f32[64,512]{1,0:T(8,128)} copy(f32[64,512]{1,0:T(8,128)} %get-tuple-element.56) | data formatting | bytes 262144

commit v3 on v0

v3 whole, which is shorter than its diff:
```python
import functools
from types import SimpleNamespace

import jax
import jax.numpy as jnp
from jax import lax
from jax.experimental import pallas as pl
from jax.experimental.pallas import tpu as pltpu
from jax.sharding import PartitionSpec as P

HEAD_SIZE = 128
NH = 2
XN = 4
EPS = 1e-6
MESH = pl.DeviceIdType.MESH
F32 = jnp.float32
BF16 = jnp.bfloat16

NN = ((1,), (0,))
NT = ((1,), (1,))
TN = ((0,), (0,))


def dg(left, right, dims):
    return lax.dot_general(left, right, (dims, ((), ())), preferred_element_type=F32)


def parts(array):
    if isinstance(array, tuple):
        return array
    if array.dtype == BF16:
        return (array,)
    high = array.astype(BF16)
    return (high, (array - high.astype(F32)).astype(BF16))


def mm(left, right, dims=NN):
    left, right = parts(left), parts(right)
    total = dg(left[0], right[0], dims)
    if len(right) > 1:
        total = total + dg(left[0], right[1], dims)
    if len(left) > 1:
        total = total + dg(left[1], right[0], dims)
    return total


def mm1(left, right, dims=NN):
    return dg(left.astype(BF16), right.astype(BF16), dims)


def order_masks(tokens):
    rows = NH * tokens
    row = lax.broadcasted_iota(jnp.int32, (rows, rows), 0)
    col = lax.broadcasted_iota(jnp.int32, (rows, rows), 1)
    row_token, col_token = row & (tokens - 1), col & (tokens - 1)
    row_step, col_step = row >= tokens, col >= tokens
    return row, col, row_token, col_token, row_step, col_step


def score_mask(tokens):
    row = lax.broadcasted_iota(jnp.int32, (tokens, NH * tokens), 0)
    col = lax.broadcasted_iota(jnp.int32, (tokens, NH * tokens), 1)
    return (col & (tokens - 1)) <= row


def unit(matrix):
    scale = lax.rsqrt(jnp.sum(matrix * matrix, axis=-1, keepdims=True) + EPS)
    return matrix * scale, scale


def layer_kernel(zn, yn, heads, names, *refs):
    r = SimpleNamespace(**dict(zip(names, refs)))
    size = HEAD_SIZE
    seq, head = lax.axis_index("seq"), lax.axis_index("head")
    z, x = lax.div(seq, XN), lax.rem(seq, XN)
    y, core = lax.div(head, 2), lax.rem(head, 2)
    above, below = lax.rem(z + 1, zn), lax.rem(z + zn - 1, zn)
    right, left, across = lax.rem(x + 1, XN), lax.rem(x + XN - 1, XN), lax.rem(x + 2, XN)
    peers = (right, left, across)
    partner = head + 1 - 2 * core
    quarter = size // XN
    count, depth = r.tok.shape
    rows = NH * count
    shard = depth // (zn * XN)
    block = r.gx.shape[1]
    width = r.g.shape[1]

    def row_device(member):
        return (z * XN + member, head)

    def remote(src, dst, send, recv, device):
        return pltpu.make_async_remote_copy(
            src_ref=src, dst_ref=dst, send_sem=send, recv_sem=recv, device_id=device, device_id_type=MESH
        )

    loads = {}
    for i, name in enumerate(("tok", "wk", "wb", "wv", "wq", "go")):
        loads[name] = pltpu.make_async_copy(getattr(r, name + "_hbm"), getattr(r, name), r.load_sem.at[i])
        loads[name].start()

    barrier = pltpu.get_barrier_semaphore()
    greeted = [row_device(peer) for peer in peers]
    greeted += [(above * XN + x, head), (below * XN + x, head), (seq, partner)]
    greeted += [(seq, lax.rem(y + d, yn) * 2 + core) for d in range(1, yn)]
    for device in greeted:
        pl.semaphore_signal(barrier, inc=1, device_id=device, device_id_type=MESH)

    loads["tok"].wait()
    for zz in range(zn):
        lanes = r.tok[:, zz * XN * shard : (zz + 1) * XN * shard]
        r.tokt[zz] = lanes.T.reshape(XN, shard, count)
    pl.semaphore_wait(barrier, len(greeted))
    own_lanes = pl.ds(pl.multiple_of(x * count, count), count)
    started = []

    def start(copy):
        copy.start()
        started.append(copy)
        return copy

    tok_copies = [
        start(remote(r.tokt.at[:, peer], r.tt.at[:, :, own_lanes], r.tsend.at[i], r.trecv.at[i], row_device(peer)))
        for i, peer in enumerate(peers)
    ]
    r.tt[:, :, own_lanes] = r.tokt[:, x]

    row, col, row_token, col_token, row_step, col_step = order_masks(count)
    strict = (col_token < row_token) | ((col_token == row_token) & row_step & ~col_step)
    smask = score_mask(count)
    loads["wk"].wait()
    loads["wb"].wait()
    tok = r.tok[...]
    pk = dg(tok, r.wk[...], NN)
    beta_all = 2.0 * jax.nn.sigmoid(dg(tok, r.wb[...], NT))
    eye = jnp.where(row == col, 1.0, 0.0)
    inverses = []
    for h in range(heads):
        base = h * NH * size
        key, key_scale = unit(jnp.concatenate([pk[:, base : base + size], pk[:, base + size : base + 2 * size]], axis=0))
        beta = jnp.concatenate([beta_all[:, 2 * h : 2 * h + 1], beta_all[:, 2 * h + 1 : 2 * h + 2]], axis=0)
        r.kr[h] = key
        r.cols[h, :, 0:1] = beta
        r.cols[h, :, 1:2] = key_scale
        system = jnp.where(strict, beta * mm(key, key, NT), 0.0)
        r.system[h] = system
        inverses.append(eye - jnp.where(col_token == row_token, system, 0.0))
    loads["wv"].wait()
    loads["wq"].wait()
    loads["go"].wait()
    pv = dg(tok, r.wv[...], NN)
    pq = dg(tok, r.wq[...], NN)
    for h in range(heads):
        base = h * NH * size
        r.vr[h] = jnp.concatenate([pv[:, base : base + size], pv[:, base + size : base + 2 * size]], axis=0)
        query, query_scale = unit(pq[:, h * size : (h + 1) * size])
        r.qr[h] = query
        r.cols[h, 0:count, 2:3] = query_scale
    level = 1
    while level < count:
        span = 2 * level - 1
        pick = ((row_token & span) >= level) & ((col_token | span) == (row_token | span)) & ((col_token & span) < level)
        for h in range(heads):
            inverse = parts(inverses[h])
            inner = mm(jnp.where(pick, r.system[h], 0.0), inverse)
            inverses[h] = inverses[h] - mm(inverse, inner)
        level *= 2
    for h in range(heads):
        key, beta = r.kr[h], r.cols[h, :, 0:1]
        query, go = r.qr[h], r.go[:, h * size : (h + 1) * size]
        inverse = parts(inverses[h])
        r.x_hi[h], r.x_lo[h] = inverse
        solved = mm(inverse, jnp.concatenate([beta * key, beta * r.vr[h]], axis=1))
        w_rows, u_rows = parts(solved[:, :size]), solved[:, size:]
        r.w_hi[h], r.w_lo[h] = w_rows
        r.ur[h] = u_rows
        key = parts(key)
        scores = jnp.where(smask, mm(query, key, NT), 0.0)
        pulled = mm(scores, go, TN)
        r.pg[h] = pulled
        r.e_own[h] = mm(key, w_rows, TN).astype(BF16)
        offset = mm(u_rows, key, TN)
        adjoint = mm(go, query, TN) - mm(pulled, w_rows, TN)
        for j in range(XN):
            r.bl_own[j, h, :quarter, :] = offset[j * quarter : (j + 1) * quarter].astype(BF16)
            r.bl_own[j, h, quarter:, :] = adjoint[j * quarter : (j + 1) * quarter].astype(BF16)

    e_right = start(remote(r.e_own, r.ebuf.at[x], r.esend.at[0], r.erecv.at[0], row_device(right)))
    e_left = start(remote(r.e_own, r.ebuf.at[x], r.esend.at[1], r.erecv.at[1], row_device(left)))
    bl_copies = [
        start(remote(r.bl_own.at[peer], r.blbuf.at[x], r.bsend.at[i], r.brecv.at[i], row_device(peer)))
        for i, peer in enumerate(peers)
    ]
    r.ebuf[x] = r.e_own[...]
    r.blbuf[x] = r.bl_own[x]

    @pl.when(z == 0)
    def _():
        r.s_in[...] = jnp.zeros_like(r.s_in)

    @pl.when(z == zn - 1)
    def _():
        r.d_in[...] = jnp.zeros_like(r.d_in)

    half = heads // 2
    e_right.wait_recv()
    spot = r.ebuf.at[left, :half]
    e_on_right = start(remote(spot, spot, r.esend.at[2], r.erecv.at[2], row_device(right)))
    e_left.wait_recv()
    spot = r.ebuf.at[right, half:]
    e_on_left = start(remote(spot, spot, r.esend.at[3], r.erecv.at[3], row_device(left)))
    for copy in bl_copies:
        copy.wait_recv()
    e_on_right.wait_recv()
    e_on_left.wait_recv()

    for h in range(heads):
        maps = [r.ebuf[j, h] for j in range(XN)]
        wide = [m.astype(F32) for m in maps]
        e10 = wide[1] + wide[0] - dg(maps[1], maps[0], NN)
        e32 = wide[3] + wide[2] - dg(maps[3], maps[2], NN)
        e10s, e32s = parts(e10), parts(e32)
        e210 = wide[2] + e10 - mm(maps[2], e10s)
        e321 = e32 + wide[1] - mm(e32s, maps[1])
        r.tot_hi[h], r.tot_lo[h] = parts(e32 + e10 - mm(e32s, e10s))
        for i, m in enumerate((maps[0], e10s[0], e210.astype(BF16))):
            r.e_pre[h, i * size : (i + 1) * size, :] = m
        for i, m in enumerate((maps[3], e32s[0], e321.astype(BF16))):
            r.e_suf[h, :, i * size : (i + 1) * size] = m
        off = r.blbuf[0, h, :quarter, :].astype(F32)
        for j in range(1, XN):
            r.s_off[j, h] = off
            off = off - mm(off, maps[j], NT) + r.blbuf[j, h, :quarter, :].astype(F32)
        r.s_off[0, h] = off
        off = r.blbuf[XN - 1, h, quarter:, :].astype(F32)
        for j in range(XN - 2, -1, -1):
            r.d_off[j, h] = off
            off = off - mm(off, maps[j], NN) + r.blbuf[j, h, quarter:, :].astype(F32)
        r.d_off[XN - 1, h] = off

    s_hop = remote(r.s_out, r.s_in, r.zsend.at[0], r.zrecv.at[0], (above * XN + x, head))
    d_hop = remote(r.d_out, r.d_in, r.zsend.at[1], r.zrecv.at[1], (below * XN + x, head))

    def hand_copy(put, got, kind, i):
        return remote(put.at[peers[i]], got.at[x], r.psend.at[i, kind], r.precv.at[i, kind], row_device(peers[i]))

    def hand_out(put, got, kind):
        for i in range(XN - 1):
            hand_copy(put, got, kind, i).start()
        got[x] = put[x]

    def forward():
        @pl.when(z > 0)
        def _():
            s_hop.wait_recv()

        @pl.when(z < zn - 1)
        def _():
            for h in range(heads):
                state = r.s_in[h]
                moved = dg(state, r.tot_hi[h], NT) + dg(state, r.tot_lo[h], NT)
                r.s_out[h] = (state.astype(F32) + r.s_off[0, h] - moved).astype(BF16)
            s_hop.start()

        for h in range(heads):
            state = r.s_in[h]
            moved = dg(state, r.e_pre[h], NT)
            r.s_put[0, h] = state
            for j in range(1, XN):
                value = state.astype(F32) + r.s_off[j, h] - moved[:, (j - 1) * size : j * size]
                r.s_put[j, h] = value.astype(BF16)
        hand_out(r.s_put, r.s_got, 0)

    def backward():
        @pl.when(z < zn - 1)
        def _():
            d_hop.wait_recv()

        @pl.when(z > 0)
        def _():
            for h in range(heads):
                state = r.d_in[h]
                moved = dg(state, r.tot_hi[h], NN) + dg(state, r.tot_lo[h], NN)
                r.d_out[h] = (state.astype(F32) + r.d_off[XN - 1, h] - moved).astype(BF16)
            d_hop.start()

        for h in range(heads):
            state = r.d_in[h]
            moved = dg(state, r.e_suf[h], NN)
            r.d_put[XN - 1, h] = state
            for j in range(XN - 1):
                i = XN - 2 - j
                value = state.astype(F32) + r.d_off[j, h] - moved[:, i * size : (i + 1) * size]
                r.d_put[j, h] = value.astype(BF16)
        hand_out(r.d_put, r.d_got, 1)

    @pl.when(z < zn // 2)
    def _():
        forward()
        backward()

    @pl.when(z >= zn // 2)
    def _():
        backward()
        forward()

    for i in range(XN - 1):
        hand_copy(r.s_put, r.s_got, 0, i).wait_recv()
        hand_copy(r.d_put, r.d_got, 1, i).wait_recv()

    two = NH * size
    value_wide = heads * two
    head_wide = size + two
    logit_at = value_wide + heads * head_wide
    cuts = [0]
    for h in range(heads):
        cuts.append(cuts[-1] + two)
    cuts += [value_wide + head_wide, value_wide + head_wide + two, width]
    cuts = list(zip(cuts[:-1], cuts[1:]))
    to_right = (True, False, True, False, False)

    def member_rows(member):
        return pl.ds(pl.multiple_of(member * count, count), count)

    def own_copy(p, way):
        lo, hi = cuts[p]
        device = row_device(left if way else right)
        src = r.g.at[:, lo:hi]
        return remote(src, r.gbuf.at[member_rows(x), lo:hi], r.gsend.at[p, way], r.grecv.at[p, way], device)

    def onward_copy(p):
        lo, hi = cuts[p]
        spot = r.gbuf.at[member_rows(left if to_right[p] else right), lo:hi]
        return remote(spot, spot, r.gsend.at[p, 2], r.grecv.at[p, 2], row_device(right if to_right[p] else left))

    def offer(p):
        lo, hi = cuts[p]
        own_copy(p, 0).start()
        own_copy(p, 1).start()
        r.gbuf[member_rows(x), lo:hi] = r.g[:, lo:hi]

    def relay(p):
        own_copy(p, 0).wait_recv()
        own_copy(p, 1).wait_recv()
        onward_copy(p).start()

    states = [jnp.concatenate([r.s_got[j, h] for j in range(XN)], axis=0) for h in range(heads)]
    adjoints = [jnp.concatenate([r.d_got[j, h] for j in range(XN)], axis=0) for h in range(heads)]
    for h in range(heads):
        keys = parts(r.kr[h])
        r.fresh[h] = r.ur[h] - mm((r.w_hi[h], r.w_lo[h]), states[h], NT)
        solved = mm((r.x_hi[h], r.x_lo[h]), r.pg[h] + mm(keys, adjoints[h], NT), TN)
        r.solved[h] = solved
        d_value = r.cols[h, :, 0:1] * solved
        for j in range(NH):
            at = h * two + j * size
            r.g[:, at : at + size] = d_value[j * count : (j + 1) * count].astype(BF16)
        offer(h)

    logits = []
    for h in range(heads):
        query, key = r.qr[h], r.kr[h]
        beta, key_scale = r.cols[h, :, 0:1], r.cols[h, :, 1:2]
        query_scale = r.cols[h, 0:count, 2:3]
        go = r.go[:, h * size : (h + 1) * size]
        solved, fresh = r.solved[h], r.fresh[h].astype(BF16)
        keys = key.astype(BF16)
        state, adjoint = states[h], adjoints[h]
        rest = r.vr[h] - dg(keys, state, NT)
        d_scores = jnp.where(smask, dg(go, fresh, NT), 0.0).astype(BF16)
        d_system = jnp.where(strict, -mm1(solved, fresh, NT), 0.0)
        gram = dg(keys, keys, NT)
        d_beta = jnp.sum(solved * rest, axis=-1, keepdims=True) + jnp.sum(d_system * gram, axis=-1, keepdims=True)
        d_gram = (beta * d_system).astype(BF16)
        d_query = dg(go, state, NN) + dg(d_scores, keys, NN)
        d_key = (
            mm1(d_scores, query, TN)
            + dg(fresh, adjoint, NN)
            - mm1(beta * solved, state)
            + dg(d_gram, keys, NN)
            + dg(d_gram, keys, TN)
        )
        d_query = query_scale * (d_query - query * jnp.sum(query * d_query, axis=-1, keepdims=True))
        d_key = key_scale * (d_key - key * jnp.sum(key * d_key, axis=-1, keepdims=True))
        d_logit = d_beta * beta * (1.0 - 0.5 * beta)
        at = value_wide + h * head_wide
        r.g[:, at : at + size] = d_query.astype(BF16)
        for j in range(NH):
            at += size
            r.g[:, at : at + size] = d_key[j * count : (j + 1) * count].astype(BF16)
            logits.append(d_logit[j * count : (j + 1) * count])
        if h == 0:
            relay(0)
            offer(heads)
    pad = jnp.zeros((count, size - len(logits)), F32)
    r.g[:, logit_at:] = jnp.concatenate(logits + [pad], axis=1).astype(BF16)
    relay(1)
    offer(heads + 1)

    def input_term(d, side):
        lo = pl.multiple_of((lax.rem(y + d, yn) * 2 + side) * block, block)
        spot = pl.ds(lo, block)
        total = dg(r.g[:, :value_wide], r.wv[spot, :], NT)
        for h in range(heads):
            at = value_wide + h * head_wide
            total = total + dg(r.g[:, at : at + size], r.wq[spot, h * size : (h + 1) * size], NT)
            total = total + dg(r.g[:, at + size : at + head_wide], r.wk[spot, h * two : (h + 1) * two], NT)
        return total + dg(r.g[:, logit_at : logit_at + heads * NH], r.wb[:, spot], NN)

    def pair_copy(d):
        return remote(r.pair_put.at[d], r.pair_got.at[d], r.csend.at[d], r.crecv.at[d], (seq, partner))

    def y_copy(d):
        i = d - 1
        device = (seq, lax.rem(y + d, yn) * 2 + core)
        return remote(r.y_put.at[i], r.y_got.at[i], r.ysend.at[i], r.yrecv.at[i], device)

    order = list(range(1, yn)) + [0]

    def partner_terms():
        for d in order:
            r.pair_put[d] = input_term(d, 1 - core).astype(BF16)
            pair_copy(d).start()

    def own_terms():
        for d in order:
            term = input_term(d, core)
            pair_copy(d).wait_recv()
            term = term + r.pair_got[d].astype(F32)
            if d:
                r.y_put[d - 1] = term.astype(BF16)
                y_copy(d).start()
            else:
                r.kept[...] = term

    def hops(p):
        return (zn // 2, zn // 2 - 1) if p % 2 == 0 else (zn // 2 - 1, zn // 2)

    def ring_hop(p, way, step):
        lo, hi = cuts[p]
        device = ((below if way else above) * XN + x, head)
        put, got = r.ring_put.at[way, step, :, lo:hi], r.ring_got.at[way, step, :, lo:hi]
        return remote(put, got, r.rsend.at[p, way, step], r.rrecv.at[p, way, step], device)

    def ring_step(p, step):
        lo, hi = cuts[p]
        if step == 0:
            onward_copy(p).wait_recv()
            left_side = r.tt[...].reshape(zn * shard, XN * count)
            r.part[:, :, lo:hi] = dg(left_side, r.gbuf[:, lo:hi], NN).reshape(zn, shard, hi - lo)
        lengths = hops(p)
        for way in range(2):
            length = lengths[way]
            if step >= length:
                continue
            chunk = lax.rem(z + zn + (step - length if way else length - step), zn)
            value = r.part[chunk, :, lo:hi]
            if step > 0:
                ring_hop(p, way, step - 1).wait_recv()
                value = value + r.ring_got[way, step - 1, :, lo:hi].astype(F32)
            r.ring_put[way, step, :, lo:hi] = value.astype(BF16)
            ring_hop(p, way, step).start()
        if step == max(lengths):
            value = r.part[z, :, lo:hi]
            for way in range(2):
                ring_hop(p, way, lengths[way] - 1).wait_recv()
                value = value + r.ring_got[way, lengths[way] - 1, :, lo:hi].astype(F32)
            r.gw[:, lo:hi] = value

    for copy in tok_copies:
        copy.wait_recv()
    delay = (0, 1, 2, 3, 3)
    extra = {0: (partner_terms, lambda: relay(2), lambda: offer(4)), 1: (own_terms, lambda: relay(3)), 2: (lambda: relay(4),)}
    for turn in range(zn // 2 + 1 + max(delay)):
        for p in range(len(cuts)):
            step = turn - delay[p]
            if 0 <= step <= zn // 2:
                ring_step(p, step)
        for action in extra.get(turn, ()):
            action()

    total = r.kept[...]
    for d in range(1, yn):
        y_copy(d).wait_recv()
        total = total + r.y_got[d - 1].astype(F32)
    r.gx[...] = total.astype(BF16)

    for copy in started:
        copy.wait_send()

    @pl.when(z < zn - 1)
    def _():
        s_hop.wait_send()

    @pl.when(z > 0)
    def _():
        d_hop.wait_send()

    for i in range(XN - 1):
        hand_copy(r.s_put, r.s_got, 0, i).wait_send()
        hand_copy(r.d_put, r.d_got, 1, i).wait_send()
    for p in range(len(cuts)):
        own_copy(p, 0).wait_send()
        own_copy(p, 1).wait_send()
        onward_copy(p).wait_send()
        for way in range(2):
            for step in range(hops(p)[way]):
                ring_hop(p, way, step).wait_send()
    for d in range(yn):
        pair_copy(d).wait_send()
        if d:
            y_copy(d).wait_send()


def finish_kernel(heads, gx_in, gw_in, gx, gwq, gwk, gwv, gwb):
    two = NH * HEAD_SIZE
    gx[...] = gx_in[...]
    gwv[...] = gw_in[:, : heads * two]
    at = heads * two
    for h in range(heads):
        gwq[:, h * HEAD_SIZE : (h + 1) * HEAD_SIZE] = gw_in[:, at : at + HEAD_SIZE]
        at += HEAD_SIZE
        gwk[:, h * two : (h + 1) * two] = gw_in[:, at : at + two]
        at += two
    gwb[...] = gw_in[:, at : at + 128].T[: heads * NH, :]


def vmem(count):
    return [pl.BlockSpec(memory_space=pltpu.VMEM)] * count


def per_device(tokens, w_query, w_key, w_value, w_beta, grad_out):
    count, depth = tokens.shape
    size = HEAD_SIZE
    heads = w_query.shape[1] // size
    rows = NH * count
    quarter = size // XN
    devices = lax.axis_size("seq")
    zn, yn = devices // XN, lax.axis_size("head") // 2
    shard, block = depth // devices, depth // (2 * yn)
    width = heads * (1 + 2 * NH) * size + 128
    pieces, hops = heads + 3, zn // 2
    w_beta_t = w_beta.T
    shape = jax.ShapeDtypeStruct
    dma = pltpu.SemaphoreType.DMA
    scratch = dict(
        tok=(tokens.shape, BF16),
        wk=(w_key.shape, BF16),
        wb=(w_beta_t.shape, BF16),
        wv=(w_value.shape, BF16),
        wq=(w_query.shape, BF16),
        go=(grad_out.shape, BF16),
        tokt=((zn, XN, shard, count), BF16),
        tt=((zn, shard, XN * count), BF16),
        system=((heads, rows, rows), F32),
        kr=((heads, rows, size), F32),
        vr=((heads, rows, size), F32),
        qr=((heads, count, size), F32),
        ur=((heads, rows, size), F32),
        pg=((heads, rows, size), F32),
        cols=((heads, rows, 8), F32),
        x_hi=((heads, rows, rows), BF16),
        x_lo=((heads, rows, rows), BF16),
        w_hi=((heads, rows, size), BF16),
        w_lo=((heads, rows, size), BF16),
        fresh=((heads, rows, size), F32),
        solved=((heads, rows, size), F32),
        e_own=((heads, size, size), BF16),
        bl_own=((XN, heads, 2 * quarter, size), BF16),
        ebuf=((XN, heads, size, size), BF16),
        blbuf=((XN, heads, 2 * quarter, size), BF16),
        tot_hi=((heads, size, size), BF16),
        tot_lo=((heads, size, size), BF16),
        e_pre=((heads, 3 * size, size), BF16),
        e_suf=((heads, size, 3 * size), BF16),
        s_off=((XN, heads, quarter, size), F32),
        d_off=((XN, heads, quarter, size), F32),
        s_in=((heads, quarter, size), BF16),
        d_in=((heads, quarter, size), BF16),
        s_out=((heads, quarter, size), BF16),
        d_out=((heads, quarter, size), BF16),
        s_put=((XN, heads, quarter, size), BF16),
        d_put=((XN, heads, quarter, size), BF16),
        s_got=((XN, heads, quarter, size), BF16),
        d_got=((XN, heads, quarter, size), BF16),
        g=((count, width), BF16),
        gbuf=((XN * count, width), BF16),
        part=((zn, shard, width), F32),
        ring_put=((2, hops, shard, width), BF16),
        ring_got=((2, hops, shard, width), BF16),
        pair_put=((yn, count, block), BF16),
        pair_got=((yn, count, block), BF16),
        y_put=((yn - 1, count, block), BF16),
        y_got=((yn - 1, count, block), BF16),
        kept=((count, block), F32),
    )
    semaphores = dict(
        load_sem=(6,),
        tsend=(XN - 1,),
        trecv=(XN - 1,),
        esend=(4,),
        erecv=(4,),
        bsend=(XN - 1,),
        brecv=(XN - 1,),
        zsend=(2,),
        zrecv=(2,),
        psend=(XN - 1, 2),
        precv=(XN - 1, 2),
        gsend=(pieces, 3),
        grecv=(pieces, 3),
        rsend=(pieces, 2, hops),
        rrecv=(pieces, 2, hops),
        csend=(yn,),
        crecv=(yn,),
        ysend=(yn - 1,),
        yrecv=(yn - 1,),
    )
    inputs = ("tok", "wq", "wk", "wv", "wb", "go")
    names = tuple(name + "_hbm" for name in inputs) + ("gx", "gw") + tuple(scratch) + tuple(semaphores)
    gx, gw = pl.pallas_call(
        functools.partial(layer_kernel, zn, yn, heads, names),
        out_shape=(shape((count, block), BF16), shape((shard, width), F32)),
        in_specs=[pl.BlockSpec(memory_space=pl.ANY)] * 6,
        out_specs=tuple(vmem(2)),
        scratch_shapes=[pltpu.VMEM(*spec) for spec in scratch.values()] + [dma(dims) for dims in semaphores.values()],
        compiler_params=pltpu.CompilerParams(collective_id=0, has_side_effects=True, vmem_limit_bytes=60 << 20),
        name="layer",
    )(tokens, w_query, w_key, w_value, w_beta_t, grad_out)
    outs = (
        shape((count, block), BF16),
        shape((shard, w_query.shape[1]), F32),
        shape((shard, w_key.shape[1]), F32),
        shape((shard, w_value.shape[1]), F32),
        shape((w_beta.shape[1], shard), F32),
    )
    grad_tokens, gwq, gwk, gwv, gwb = pl.pallas_call(
        functools.partial(finish_kernel, heads),
        out_shape=outs,
        in_specs=vmem(2),
        out_specs=tuple(vmem(5)),
        name="finish",
    )(gx, gw)
    return (grad_tokens, gwq, gwk, gwv, gwb.T)


def solution(mesh):
    in_specs = (
        P("seq", None),
        P(None, "head"),
        P(None, "head"),
        P(None, "head"),
        P(None, "head"),
        P("seq", "head"),
    )
    return jax.shard_map(
        per_device, mesh=mesh, in_specs=in_specs, out_specs=(P("seq", "head"),) * 5, check_vma=False
    )
```

time: 1260 us -> 89.4 us (0.07)
  waiting for transfers between devices: 747 us -> 0 us
  other arithmetic: 176 us -> 0 us
  starting transfers between devices: 152 us -> 0 us
  matrix products: 119 us -> 0 us
  Pallas kernels: 0 us -> 87.7 us
  local copies, waits for them, and re-layouts: 49.4 us -> 0 us
  between operations: 14.5 us -> 0.64 us
    ppermute x62 -> x0, waiting for transfers between devices: 450 us -> none  [passed_along(): return lax.ppermute(array, axis, pairs)]
    unnamed x3 -> x0, waiting for transfers between devices: 265 us -> none
    another operation x28 -> x0, other arithmetic: 164 us -> none  [block_weights(): lax.linalg.triangular_solve(system, jnp.diag(beta_rows), left_side=True,...]
    ppermute x62 -> x0, starting transfers between devices: 152 us -> none  [passed_along(): return lax.ppermute(array, axis, pairs)]
    dot_general x145 -> x0, matrix products: 109 us -> none  [the longest x72 55.3 us: product(): return jnp.matmul(left, right, precision=highest)]
    pallas_call x0 -> x2, Pallas kernels: none -> 87.7 us  [the longest x1 85.9 us: per_device(): pl.pallas_call(functools.partial(layer_kernel, zn, yn, heads, names), out...]
    reduce_scatter x1 -> x0, waiting for transfers between devices: 32.1 us -> none  [per_device(): lax.psum_scatter(input_term.astype(jnp.bfloat16), 'head', scatter_dimensi...]
    unnamed x49 -> x0, local copies, waits for them, and re-layouts: 16.3 us -> none
  transfers between devices with their start and end apart: 64 -> 0, of which waited for: 64 -> 0; matrix products, arithmetic and copies ran while one was open for 1% -> 0% of each run, Pallas kernels for 0% -> 0%
where the time goes in v3:
time: 89.4 us; the launch traced here: 88.3 us
  Pallas kernels  87.7 us (98%)
    pallas_call x1, Pallas kernels, per_device(): pl.pallas_call(functools.partial(layer_kernel, zn, yn, heads, names), out...  85.9 us

profile of v3, /device:TPU:32, one launch (start us, length us, event | category | flops | bytes accessed | tf_op | source)
XLA Modules:
  0.0 88.3 jit_solution(3641775518321429272)
XLA Ops:
  0.6 85.9 %layer.1 = (bf16[128,256]{1,0:T(8,128)(2,1)}, f32[64,1408]{1,0:T(8,128)}) custom-call(bf16[128,2048]{1,0:T(8,128)(2,1)} %refs_0_.1, bf16[2048,256]{1,0:T(8,128)(2,1)} %refs_1_.1, bf16[2048,512]{1,0:T(8,128)(2,1)} %refs_2_.1, bf16[2048,512]{1,0:T(8,128)(2,1)} %refs_3_.1, bf16[4,2048]{1,0:T(4,128)(2,1)} %bitcast.2, bf16[128,256]{1,0:T(8,128)(2,1)} %refs_5_.1), custom_call_target="tpu_custom_call" | custom-call | tf_op jit(solution)/shard_map/layer/pallas_call | solution.py:619
  86.5 1.8 %finish.1 = (bf16[128,256]{1,0:T(8,128)(2,1)}, f32[64,256]{1,0:T(8,128)}, f32[64,512]{1,0:T(8,128)}, f32[64,512]{1,0:T(8,128)}, f32[4,64]{1,0:T(4,128)}) custom-call(bf16[128,256]{1,0:T(8,128)(2,1)} %get-tuple-element.12.gx_in, f32[64,1408]{1,0:T(8,128)} %get-tuple-element.13.gw_in), custom_call_target="tpu_custom_call" | custom-call | tf_op jit(solution)/shard_map/finish/pallas_call | solution.py:635

commit v4 on v3

--- a/solution.py
+++ b/solution.py
@@ -75,6 +75,9 @@
     z, x = lax.div(seq, XN), lax.rem(seq, XN)
     y, core = lax.div(head, 2), lax.rem(head, 2)
     above, below = lax.rem(z + 1, zn), lax.rem(z + zn - 1, zn)
+    odd = lax.rem(z, 2)
+    beside = z + 1 - 2 * odd
+    above2, below2 = lax.rem(z + 2, zn), lax.rem(z + zn - 2, zn)
     right, left, across = lax.rem(x + 1, XN), lax.rem(x + XN - 1, XN), lax.rem(x + 2, XN)
     peers = (right, left, across)
     partner = head + 1 - 2 * core
@@ -100,7 +103,7 @@
 
     barrier = pltpu.get_barrier_semaphore()
     greeted = [row_device(peer) for peer in peers]
-    greeted += [(above * XN + x, head), (below * XN + x, head), (seq, partner)]
+    greeted += [(zz * XN + x, head) for zz in (above, below, above2, below2)] + [(seq, partner)]
     greeted += [(seq, lax.rem(y + d, yn) * 2 + core) for d in range(1, yn)]
     for device in greeted:
         pl.semaphore_signal(barrier, inc=1, device_id=device, device_id_type=MESH)
@@ -109,7 +112,6 @@
     for zz in range(zn):
         lanes = r.tok[:, zz * XN * shard : (zz + 1) * XN * shard]
         r.tokt[zz] = lanes.T.reshape(XN, shard, count)
-    pl.semaphore_wait(barrier, len(greeted))
     own_lanes = pl.ds(pl.multiple_of(x * count, count), count)
     started = []
 
@@ -117,12 +119,6 @@
         copy.start()
         started.append(copy)
         return copy
-
-    tok_copies = [
-        start(remote(r.tokt.at[:, peer], r.tt.at[:, :, own_lanes], r.tsend.at[i], r.trecv.at[i], row_device(peer)))
-        for i, peer in enumerate(peers)
-    ]
-    r.tt[:, :, own_lanes] = r.tokt[:, x]
 
     row, col, row_token, col_token, row_step, col_step = order_masks(count)
     strict = (col_token < row_token) | ((col_token == row_token) & row_step & ~col_step)
@@ -184,6 +180,7 @@
             r.bl_own[j, h, :quarter, :] = offset[j * quarter : (j + 1) * quarter].astype(BF16)
             r.bl_own[j, h, quarter:, :] = adjoint[j * quarter : (j + 1) * quarter].astype(BF16)
 
+    pl.semaphore_wait(barrier, len(greeted))
     e_right = start(remote(r.e_own, r.ebuf.at[x], r.esend.at[0], r.erecv.at[0], row_device(right)))
     e_left = start(remote(r.e_own, r.ebuf.at[x], r.esend.at[1], r.erecv.at[1], row_device(left)))
     bl_copies = [
@@ -193,11 +190,11 @@
     r.ebuf[x] = r.e_own[...]
     r.blbuf[x] = r.bl_own[x]
 
-    @pl.when(z == 0)
+    @pl.when(z < 2)
     def _():
         r.s_in[...] = jnp.zeros_like(r.s_in)
 
-    @pl.when(z == zn - 1)
+    @pl.when(z >= zn - 2)
     def _():
         r.d_in[...] = jnp.zeros_like(r.d_in)
 
@@ -212,6 +209,11 @@
         copy.wait_recv()
     e_on_right.wait_recv()
     e_on_left.wait_recv()
+    tok_copies = [
+        start(remote(r.tokt.at[:, peer], r.tt.at[:, :, own_lanes], r.tsend.at[i], r.trecv.at[i], row_device(peer)))
+        for i, peer in enumerate(peers)
+    ]
+    r.tt[:, :, own_lanes] = r.tokt[:, x]
 
     for h in range(heads):
         maps = [r.ebuf[j, h] for j in range(XN)]
@@ -221,7 +223,7 @@
         e10s, e32s = parts(e10), parts(e32)
         e210 = wide[2] + e10 - mm(maps[2], e10s)
         e321 = e32 + wide[1] - mm(e32s, maps[1])
-        r.tot_hi[h], r.tot_lo[h] = parts(e32 + e10 - mm(e32s, e10s))
+        r.fz[odd, h] = (e32 + e10 - mm(e32s, e10s)).astype(BF16)
         for i, m in enumerate((maps[0], e10s[0], e210.astype(BF16))):
             r.e_pre[h, i * size : (i + 1) * size, :] = m
         for i, m in enumerate((maps[3], e32s[0], e321.astype(BF16))):
@@ -230,15 +232,30 @@
         for j in range(1, XN):
             r.s_off[j, h] = off
             off = off - mm(off, maps[j], NT) + r.blbuf[j, h, :quarter, :].astype(F32)
-        r.s_off[0, h] = off
+        r.sz[odd, h] = off.astype(BF16)
         off = r.blbuf[XN - 1, h, quarter:, :].astype(F32)
         for j in range(XN - 2, -1, -1):
             r.d_off[j, h] = off
             off = off - mm(off, maps[j], NN) + r.blbuf[j, h, quarter:, :].astype(F32)
-        r.d_off[XN - 1, h] = off
-
-    s_hop = remote(r.s_out, r.s_in, r.zsend.at[0], r.zrecv.at[0], (above * XN + x, head))
-    d_hop = remote(r.d_out, r.d_in, r.zsend.at[1], r.zrecv.at[1], (below * XN + x, head))
+        r.dz[odd, h] = off.astype(BF16)
+
+    pair_swaps = [
+        start(remote(ref.at[odd], ref.at[odd], r.swap_send.at[i], r.swap_recv.at[i], (beside * XN + x, head)))
+        for i, ref in enumerate((r.fz, r.sz, r.dz))
+    ]
+    for copy in pair_swaps:
+        copy.wait_recv()
+    for h in range(heads):
+        low, high = r.fz[0, h], r.fz[1, h]
+        both = high.astype(F32) + low.astype(F32) - dg(high, low, NN)
+        r.pair[h] = both.astype(BF16)
+        r.pair_t[h] = both.T.astype(BF16)
+        s_low, d_high = r.sz[0, h], r.dz[1, h]
+        r.s_off[0, h] = s_low.astype(F32) - dg(s_low, high, NT) + r.sz[1, h].astype(F32)
+        r.d_off[XN - 1, h] = d_high.astype(F32) - dg(d_high, low, NN) + r.dz[0, h].astype(F32)
+
+    s_hop = remote(r.s_out, r.s_in, r.zsend.at[0], r.zrecv.at[0], (above2 * XN + x, head))
+    d_hop = remote(r.d_out, r.d_in, r.zsend.at[1], r.zrecv.at[1], (below2 * XN + x, head))
 
     def hand_copy(put, got, kind, i):
         return remote(put.at[peers[i]], got.at[x], r.psend.at[i, kind], r.precv.at[i, kind], row_device(peers[i]))
@@ -249,20 +266,31 @@
         got[x] = put[x]
 
     def forward():
-        @pl.when(z > 0)
+        @pl.when(z >= 2)
         def _():
             s_hop.wait_recv()
 
-        @pl.when(z < zn - 1)
+        @pl.when(z < zn - 2)
         def _():
             for h in range(heads):
                 state = r.s_in[h]
-                moved = dg(state, r.tot_hi[h], NT) + dg(state, r.tot_lo[h], NT)
+                moved = dg(state, r.pair_t[h], NN)
                 r.s_out[h] = (state.astype(F32) + r.s_off[0, h] - moved).astype(BF16)
             s_hop.start()
 
+        @pl.when(odd == 0)
+        def _():
+            r.s_mine[...] = r.s_in[...]
+
+        @pl.when(odd == 1)
+        def _():
+            for h in range(heads):
+                state = r.s_in[h]
+                moved = dg(state, r.fz[0, h], NT)
+                r.s_mine[h] = (state.astype(F32) + r.sz[0, h].astype(F32) - moved).astype(BF16)
+
         for h in range(heads):
-            state = r.s_in[h]
+            state = r.s_mine[h]
             moved = dg(state, r.e_pre[h], NT)
             r.s_put[0, h] = state
             for j in range(1, XN):
@@ -271,20 +299,31 @@
         hand_out(r.s_put, r.s_got, 0)
 
     def backward():
-        @pl.when(z < zn - 1)
+        @pl.when(z < zn - 2)
         def _():
             d_hop.wait_recv()
 
-        @pl.when(z > 0)
+        @pl.when(z >= 2)
         def _():
             for h in range(heads):
                 state = r.d_in[h]
-                moved = dg(state, r.tot_hi[h], NN) + dg(state, r.tot_lo[h], NN)
+                moved = dg(state, r.pair[h], NN)
                 r.d_out[h] = (state.astype(F32) + r.d_off[XN - 1, h] - moved).astype(BF16)
             d_hop.start()
 
+        @pl.when(odd == 1)
+        def _():
+            r.d_mine[...] = r.d_in[...]
+
+        @pl.when(odd == 0)
+        def _():
+            for h in range(heads):
+                state = r.d_in[h]
+                moved = dg(state, r.fz[1, h], NN)
+                r.d_mine[h] = (state.astype(F32) + r.dz[1, h].astype(F32) - moved).astype(BF16)
+
         for h in range(heads):
-            state = r.d_in[h]
+            state = r.d_mine[h]
             moved = dg(state, r.e_suf[h], NN)
             r.d_put[XN - 1, h] = state
             for j in range(XN - 1):
@@ -389,12 +428,9 @@
             r.g[:, at : at + size] = d_key[j * count : (j + 1) * count].astype(BF16)
             logits.append(d_logit[j * count : (j + 1) * count])
         if h == 0:
-            relay(0)
             offer(heads)
     pad = jnp.zeros((count, size - len(logits)), F32)
     r.g[:, logit_at:] = jnp.concatenate(logits + [pad], axis=1).astype(BF16)
-    relay(1)
-    offer(heads + 1)
 
     def input_term(d, side):
         lo = pl.multiple_of((lax.rem(y + d, yn) * 2 + side) * block, block)
@@ -466,17 +502,30 @@
                 value = value + r.ring_got[way, lengths[way] - 1, :, lo:hi].astype(F32)
             r.gw[:, lo:hi] = value
 
+    partner_terms()
+    relay(0)
+    relay(1)
+    offer(3)
+    offer(4)
+    own_terms()
+    relay(2)
     for copy in tok_copies:
         copy.wait_recv()
-    delay = (0, 1, 2, 3, 3)
-    extra = {0: (partner_terms, lambda: relay(2), lambda: offer(4)), 1: (own_terms, lambda: relay(3)), 2: (lambda: relay(4),)}
-    for turn in range(zn // 2 + 1 + max(delay)):
-        for p in range(len(cuts)):
-            step = turn - delay[p]
-            if 0 <= step <= zn // 2:
-                ring_step(p, step)
-        for action in extra.get(turn, ()):
-            action()
+    ring_step(0, 0)
+    ring_step(1, 0)
+    relay(3)
+    relay(4)
+    ring_step(0, 1)
+    ring_step(1, 1)
+    for p in (3, 2, 4):
+        ring_step(p, 0)
+    for step in range(2, zn // 2 + 1):
+        for p in (0, 1):
+            ring_step(p, step)
+        for p in (3, 2, 4):
+            ring_step(p, step - 1)
+    for p in (3, 2, 4):
+        ring_step(p, zn // 2)
 
     total = r.kept[...]
     for d in range(1, yn):
@@ -487,11 +536,11 @@
     for copy in started:
         copy.wait_send()
 
-    @pl.when(z < zn - 1)
+    @pl.when(z < zn - 2)
     def _():
         s_hop.wait_send()
 
-    @pl.when(z > 0)
+    @pl.when(z >= 2)
     def _():
         d_hop.wait_send()
 
@@ -568,8 +617,13 @@
         bl_own=((XN, heads, 2 * quarter, size), BF16),
         ebuf=((XN, heads, size, size), BF16),
         blbuf=((XN, heads, 2 * quarter, size), BF16),
-        tot_hi=((heads, size, size), BF16),
-        tot_lo=((heads, size, size), BF16),
+        fz=((2, heads, size, size), BF16),
+        sz=((2, heads, quarter, size), BF16),
+        dz=((2, heads, quarter, size), BF16),
+        pair=((heads, size, size), BF16),
+        pair_t=((heads, size, size), BF16),
+        s_mine=((heads, quarter, size), BF16),
+        d_mine=((heads, quarter, size), BF16),
         e_pre=((heads, 3 * size, size), BF16),
         e_suf=((heads, size, 3 * size), BF16),
         s_off=((XN, heads, quarter, size), F32),
@@ -601,6 +655,8 @@
         erecv=(4,),
         bsend=(XN - 1,),
         brecv=(XN - 1,),
+        swap_send=(3,),
+        swap_recv=(3,),
         zsend=(2,),
         zrecv=(2,),
         psend=(XN - 1, 2),

time: 89.4 us -> 76.1 us (0.85)
  Pallas kernels: 87.7 us -> 74.9 us
    pallas_call x1, Pallas kernels: 85.9 us -> 73.1 us  [per_device(): pl.pallas_call(functools.partial(layer_kernel, zn, yn, heads, names), out...]
where the time goes in v4:
time: 76.1 us; the launch traced here: 75.5 us
  Pallas kernels  74.9 us (98%)
    pallas_call x1, Pallas kernels, per_device(): pl.pallas_call(functools.partial(layer_kernel, zn, yn, heads, names), out...  73.1 us
    pallas_call x1, Pallas kernels, per_device(): pl.pallas_call(functools.partial(finish_kernel, heads), out_shape=outs, i...  1.77 us

profile of v4, /device:TPU:32, one launch (start us, length us, event | category | flops | bytes accessed | tf_op | source)
XLA Modules:
  0.0 75.5 jit_solution(18042021894216305137)
XLA Ops:
  0.6 73.1 %layer.1 = (bf16[128,256]{1,0:T(8,128)(2,1)}, f32[64,1408]{1,0:T(8,128)}) custom-call(bf16[128,2048]{1,0:T(8,128)(2,1)} %refs_0_.1, bf16[2048,256]{1,0:T(8,128)(2,1)} %refs_1_.1, bf16[2048,512]{1,0:T(8,128)(2,1)} %refs_2_.1, bf16[2048,512]{1,0:T(8,128)(2,1)} %refs_3_.1, bf16[4,2048]{1,0:T(4,128)(2,1)} %bitcast.2, bf16[128,256]{1,0:T(8,128)(2,1)} %refs_5_.1), custom_call_target="tpu_custom_call" | custom-call | tf_op jit(solution)/shard_map/layer/pallas_call | solution.py:675
  73.7 1.8 %finish.1 = (bf16[128,256]{1,0:T(8,128)(2,1)}, f32[64,256]{1,0:T(8,128)}, f32[64,512]{1,0:T(8,128)}, f32[64,512]{1,0:T(8,128)}, f32[4,64]{1,0:T(4,128)}) custom-call(bf16[128,256]{1,0:T(8,128)(2,1)} %get-tuple-element.12.gx_in, f32[64,1408]{1,0:T(8,128)} %get-tuple-element.13.gw_in), custom_call_target="tpu_custom_call" | custom-call | tf_op jit(solution)/shard_map/finish/pallas_call | solution.py:691

commit v5 on v4

--- a/solution.py
+++ b/solution.py
@@ -109,9 +109,6 @@
         pl.semaphore_signal(barrier, inc=1, device_id=device, device_id_type=MESH)
 
     loads["tok"].wait()
-    for zz in range(zn):
-        lanes = r.tok[:, zz * XN * shard : (zz + 1) * XN * shard]
-        r.tokt[zz] = lanes.T.reshape(XN, shard, count)
     own_lanes = pl.ds(pl.multiple_of(x * count, count), count)
     started = []
 
@@ -160,29 +157,33 @@
             inner = mm(jnp.where(pick, r.system[h], 0.0), inverse)
             inverses[h] = inverses[h] - mm(inverse, inner)
         level *= 2
+    e_copies = {}
     for h in range(heads):
         key, beta = r.kr[h], r.cols[h, :, 0:1]
-        query, go = r.qr[h], r.go[:, h * size : (h + 1) * size]
         inverse = parts(inverses[h])
         r.x_hi[h], r.x_lo[h] = inverse
         solved = mm(inverse, jnp.concatenate([beta * key, beta * r.vr[h]], axis=1))
-        w_rows, u_rows = parts(solved[:, :size]), solved[:, size:]
+        w_rows = parts(solved[:, :size])
         r.w_hi[h], r.w_lo[h] = w_rows
-        r.ur[h] = u_rows
-        key = parts(key)
+        r.ur[h] = solved[:, size:]
+        r.e_own[h] = mm(key, w_rows, TN).astype(BF16)
+        if h == 0:
+            pl.semaphore_wait(barrier, len(greeted))
+        for way, device in enumerate((right, left)):
+            e_copies[h, way] = start(
+                remote(r.e_own.at[h], r.ebuf.at[x, h], r.esend.at[h, way], r.erecv.at[h, way], row_device(device))
+            )
+    for h in range(heads):
+        query, go = r.qr[h], r.go[:, h * size : (h + 1) * size]
+        key = parts(r.kr[h])
         scores = jnp.where(smask, mm(query, key, NT), 0.0)
         pulled = mm(scores, go, TN)
         r.pg[h] = pulled
-        r.e_own[h] = mm(key, w_rows, TN).astype(BF16)
-        offset = mm(u_rows, key, TN)
-        adjoint = mm(go, query, TN) - mm(pulled, w_rows, TN)
+        offset = mm(r.ur[h], key, TN)
+        adjoint = mm(go, query, TN) - mm(pulled, (r.w_hi[h], r.w_lo[h]), TN)
         for j in range(XN):
             r.bl_own[j, h, :quarter, :] = offset[j * quarter : (j + 1) * quarter].astype(BF16)
             r.bl_own[j, h, quarter:, :] = adjoint[j * quarter : (j + 1) * quarter].astype(BF16)
-
-    pl.semaphore_wait(barrier, len(greeted))
-    e_right = start(remote(r.e_own, r.ebuf.at[x], r.esend.at[0], r.erecv.at[0], row_device(right)))
-    e_left = start(remote(r.e_own, r.ebuf.at[x], r.esend.at[1], r.erecv.at[1], row_device(left)))
     bl_copies = [
         start(remote(r.bl_own.at[peer], r.blbuf.at[x], r.bsend.at[i], r.brecv.at[i], row_device(peer)))
         for i, peer in enumerate(peers)
@@ -198,17 +199,21 @@
     def _():
         r.d_in[...] = jnp.zeros_like(r.d_in)
 
-    half = heads // 2
-    e_right.wait_recv()
-    spot = r.ebuf.at[left, :half]
-    e_on_right = start(remote(spot, spot, r.esend.at[2], r.erecv.at[2], row_device(right)))
-    e_left.wait_recv()
-    spot = r.ebuf.at[right, half:]
-    e_on_left = start(remote(spot, spot, r.esend.at[3], r.erecv.at[3], row_device(left)))
+    e_onward = []
+    for h in range(heads):
+        for way in range(2):
+            e_copies[h, way].wait_recv()
+        to_right = h < heads // 2
+        spot = r.ebuf.at[left if to_right else right, h]
+        device = row_device(right if to_right else left)
+        e_onward.append(start(remote(spot, spot, r.esend.at[h, 2], r.erecv.at[h, 2], device)))
+    for zz in range(zn):
+        lanes = r.tok[:, zz * XN * shard : (zz + 1) * XN * shard]
+        r.tokt[zz] = lanes.T.reshape(XN, shard, count)
     for copy in bl_copies:
         copy.wait_recv()
-    e_on_right.wait_recv()
-    e_on_left.wait_recv()
+    for copy in e_onward:
+        copy.wait_recv()
     tok_copies = [
         start(remote(r.tokt.at[:, peer], r.tt.at[:, :, own_lanes], r.tsend.at[i], r.trecv.at[i], row_device(peer)))
         for i, peer in enumerate(peers)
@@ -332,30 +337,13 @@
                 r.d_put[j, h] = value.astype(BF16)
         hand_out(r.d_put, r.d_got, 1)
 
-    @pl.when(z < zn // 2)
-    def _():
-        forward()
-        backward()
-
-    @pl.when(z >= zn // 2)
-    def _():
-        backward()
-        forward()
-
-    for i in range(XN - 1):
-        hand_copy(r.s_put, r.s_got, 0, i).wait_recv()
-        hand_copy(r.d_put, r.d_got, 1, i).wait_recv()
-
     two = NH * size
-    value_wide = heads * two
-    head_wide = size + two
-    logit_at = value_wide + heads * head_wide
-    cuts = [0]
-    for h in range(heads):
-        cuts.append(cuts[-1] + two)
-    cuts += [value_wide + head_wide, value_wide + head_wide + two, width]
+    value_at = heads * size
+    key_at = value_at + heads * two
+    logit_at = key_at + heads * two
+    cuts = [0, value_at] + [value_at + (h + 1) * two for h in range(heads)] + [logit_at - size, width]
     cuts = list(zip(cuts[:-1], cuts[1:]))
-    to_right = (True, False, True, False, False)
+    to_right = (True, False, True, False, True)
 
     def member_rows(member):
         return pl.ds(pl.multiple_of(member * count, count), count)
@@ -382,64 +370,87 @@
         own_copy(p, 1).wait_recv()
         onward_copy(p).start()
 
-    states = [jnp.concatenate([r.s_got[j, h] for j in range(XN)], axis=0) for h in range(heads)]
-    adjoints = [jnp.concatenate([r.d_got[j, h] for j in range(XN)], axis=0) for h in range(heads)]
+    def joined(got, h):
+        return jnp.concatenate([got[j, h] for j in range(XN)], axis=0)
+
+    def query_grads():
+        for i in range(XN - 1):
+            hand_copy(r.s_put, r.s_got, 0, i).wait_recv()
+        for h in range(heads):
+            state = joined(r.s_got, h)
+            keys, query = r.kr[h].astype(BF16), r.qr[h]
+            go = r.go[:, h * size : (h + 1) * size]
+            fresh = (r.ur[h] - mm((r.w_hi[h], r.w_lo[h]), state, NT)).astype(BF16)
+            r.fresh[h] = fresh
+            d_scores = jnp.where(smask, dg(go, fresh, NT), 0.0).astype(BF16)
+            d_query = dg(go, state, NN) + dg(d_scores, keys, NN)
+            d_query = r.cols[h, 0:count, 2:3] * (d_query - query * jnp.sum(query * d_query, axis=-1, keepdims=True))
+            r.g[:, h * size : (h + 1) * size] = d_query.astype(BF16)
+            if h == heads - 1:
+                offer(0)
+            r.rest[h] = r.vr[h] - dg(keys, state, NT)
+            r.dk[h] = mm1(d_scores, query, TN)
+
+    early = z < zn // 2
+
+    @pl.when(early)
+    def _():
+        forward()
+        query_grads()
+        backward()
+        relay(0)
+
+    @pl.when(jnp.logical_not(early))
+    def _():
+        backward()
+        forward()
+        query_grads()
+
+    for i in range(XN - 1):
+        hand_copy(r.d_put, r.d_got, 1, i).wait_recv()
+    adjoints = [joined(r.d_got, h) for h in range(heads)]
     for h in range(heads):
         keys = parts(r.kr[h])
-        r.fresh[h] = r.ur[h] - mm((r.w_hi[h], r.w_lo[h]), states[h], NT)
         solved = mm((r.x_hi[h], r.x_lo[h]), r.pg[h] + mm(keys, adjoints[h], NT), TN)
         r.solved[h] = solved
         d_value = r.cols[h, :, 0:1] * solved
         for j in range(NH):
-            at = h * two + j * size
+            at = value_at + h * two + j * size
             r.g[:, at : at + size] = d_value[j * count : (j + 1) * count].astype(BF16)
-        offer(h)
+        offer(1 + h)
 
     logits = []
     for h in range(heads):
-        query, key = r.qr[h], r.kr[h]
+        key = r.kr[h]
         beta, key_scale = r.cols[h, :, 0:1], r.cols[h, :, 1:2]
-        query_scale = r.cols[h, 0:count, 2:3]
-        go = r.go[:, h * size : (h + 1) * size]
-        solved, fresh = r.solved[h], r.fresh[h].astype(BF16)
-        keys = key.astype(BF16)
-        state, adjoint = states[h], adjoints[h]
-        rest = r.vr[h] - dg(keys, state, NT)
-        d_scores = jnp.where(smask, dg(go, fresh, NT), 0.0).astype(BF16)
+        solved, fresh, keys = r.solved[h], r.fresh[h], key.astype(BF16)
         d_system = jnp.where(strict, -mm1(solved, fresh, NT), 0.0)
         gram = dg(keys, keys, NT)
-        d_beta = jnp.sum(solved * rest, axis=-1, keepdims=True) + jnp.sum(d_system * gram, axis=-1, keepdims=True)
+        d_beta = jnp.sum(solved * r.rest[h], axis=-1, keepdims=True) + jnp.sum(d_system * gram, axis=-1, keepdims=True)
         d_gram = (beta * d_system).astype(BF16)
-        d_query = dg(go, state, NN) + dg(d_scores, keys, NN)
         d_key = (
-            mm1(d_scores, query, TN)
-            + dg(fresh, adjoint, NN)
-            - mm1(beta * solved, state)
+            r.dk[h]
+            + dg(fresh, adjoints[h], NN)
+            - mm1(beta * solved, joined(r.s_got, h))
             + dg(d_gram, keys, NN)
             + dg(d_gram, keys, TN)
         )
-        d_query = query_scale * (d_query - query * jnp.sum(query * d_query, axis=-1, keepdims=True))
         d_key = key_scale * (d_key - key * jnp.sum(key * d_key, axis=-1, keepdims=True))
         d_logit = d_beta * beta * (1.0 - 0.5 * beta)
-        at = value_wide + h * head_wide
-        r.g[:, at : at + size] = d_query.astype(BF16)
         for j in range(NH):
-            at += size
+            at = key_at + h * two + j * size
             r.g[:, at : at + size] = d_key[j * count : (j + 1) * count].astype(BF16)
             logits.append(d_logit[j * count : (j + 1) * count])
-        if h == 0:
-            offer(heads)
     pad = jnp.zeros((count, size - len(logits)), F32)
     r.g[:, logit_at:] = jnp.concatenate(logits + [pad], axis=1).astype(BF16)
+    offer(3)
 
     def input_term(d, side):
         lo = pl.multiple_of((lax.rem(y + d, yn) * 2 + side) * block, block)
         spot = pl.ds(lo, block)
-        total = dg(r.g[:, :value_wide], r.wv[spot, :], NT)
-        for h in range(heads):
-            at = value_wide + h * head_wide
-            total = total + dg(r.g[:, at : at + size], r.wq[spot, h * size : (h + 1) * size], NT)
-            total = total + dg(r.g[:, at + size : at + head_wide], r.wk[spot, h * two : (h + 1) * two], NT)
+        total = dg(r.g[:, :value_at], r.wq[spot, :], NT)
+        total = total + dg(r.g[:, value_at:key_at], r.wv[spot, :], NT)
+        total = total + dg(r.g[:, key_at:logit_at], r.wk[spot, :], NT)
         return total + dg(r.g[:, logit_at : logit_at + heads * NH], r.wb[:, spot], NN)
 
     def pair_copy(d):
@@ -459,9 +470,12 @@
 
     def own_terms():
         for d in order:
-            term = input_term(d, core)
+            r.own_part[d] = input_term(d, core)
+
+    def merge_terms():
+        for d in order:
             pair_copy(d).wait_recv()
-            term = term + r.pair_got[d].astype(F32)
+            term = r.own_part[d] + r.pair_got[d].astype(F32)
             if d:
                 r.y_put[d - 1] = term.astype(BF16)
                 y_copy(d).start()
@@ -502,29 +516,34 @@
                 value = value + r.ring_got[way, lengths[way] - 1, :, lo:hi].astype(F32)
             r.gw[:, lo:hi] = value
 
+    @pl.when(jnp.logical_not(early))
+    def _():
+        relay(0)
+
     partner_terms()
-    relay(0)
     relay(1)
-    offer(3)
+    relay(2)
     offer(4)
-    own_terms()
-    relay(2)
     for copy in tok_copies:
         copy.wait_recv()
     ring_step(0, 0)
+    own_terms()
+    relay(3)
     ring_step(1, 0)
-    relay(3)
+    ring_step(2, 0)
     relay(4)
-    ring_step(0, 1)
-    ring_step(1, 1)
-    for p in (3, 2, 4):
-        ring_step(p, 0)
+    for p in (0, 1, 2):
+        ring_step(p, 1)
+    ring_step(3, 0)
+    ring_step(4, 0)
     for step in range(2, zn // 2 + 1):
-        for p in (0, 1):
+        for p in (0, 1, 2):
             ring_step(p, step)
-        for p in (3, 2, 4):
+        if step == zn // 2:
+            merge_terms()
+        for p in (3, 4):
             ring_step(p, step - 1)
-    for p in (3, 2, 4):
+    for p in (3, 4):
         ring_step(p, zn // 2)
 
     total = r.kept[...]
@@ -561,15 +580,12 @@
 
 
 def finish_kernel(heads, gx_in, gw_in, gx, gwq, gwk, gwv, gwb):
-    two = NH * HEAD_SIZE
+    queries, steps = heads * HEAD_SIZE, heads * NH * HEAD_SIZE
     gx[...] = gx_in[...]
-    gwv[...] = gw_in[:, : heads * two]
-    at = heads * two
-    for h in range(heads):
-        gwq[:, h * HEAD_SIZE : (h + 1) * HEAD_SIZE] = gw_in[:, at : at + HEAD_SIZE]
-        at += HEAD_SIZE
-        gwk[:, h * two : (h + 1) * two] = gw_in[:, at : at + two]
-        at += two
+    gwq[...] = gw_in[:, :queries]
+    gwv[...] = gw_in[:, queries : queries + steps]
+    gwk[...] = gw_in[:, queries + steps : queries + 2 * steps]
+    at = queries + 2 * steps
     gwb[...] = gw_in[:, at : at + 128].T[: heads * NH, :]
 
 
@@ -611,7 +627,9 @@
         x_lo=((heads, rows, rows), BF16),
         w_hi=((heads, rows, size), BF16),
         w_lo=((heads, rows, size), BF16),
-        fresh=((heads, rows, size), F32),
+        fresh=((heads, rows, size), BF16),
+        rest=((heads, rows, size), F32),
+        dk=((heads, rows, size), F32),
         solved=((heads, rows, size), F32),
         e_own=((heads, size, size), BF16),
         bl_own=((XN, heads, 2 * quarter, size), BF16),
@@ -645,14 +663,15 @@
         pair_got=((yn, count, block), BF16),
         y_put=((yn - 1, count, block), BF16),
         y_got=((yn - 1, count, block), BF16),
+        own_part=((yn, count, block), F32),
         kept=((count, block), F32),
     )
     semaphores = dict(
         load_sem=(6,),
         tsend=(XN - 1,),
         trecv=(XN - 1,),
-        esend=(4,),
-        erecv=(4,),
+        esend=(heads, 3),
+        erecv=(heads, 3),
         bsend=(XN - 1,),
         brecv=(XN - 1,),
         swap_send=(3,),

time: 76.1 us -> 74 us (0.972)
  Pallas kernels: 74.9 us -> 73.3 us
    pallas_call x1, Pallas kernels: 73.1 us -> 71.5 us  [per_device(): pl.pallas_call(functools.partial(layer_kernel, zn, yn, heads, names), out...]
where the time goes in v5:
time: 74 us; the launch traced here: 73.9 us
  Pallas kernels  73.3 us (99%)
    pallas_call x1, Pallas kernels, per_device(): pl.pallas_call(functools.partial(layer_kernel, zn, yn, heads, names), out...  71.5 us
    pallas_call x1, Pallas kernels, per_device(): pl.pallas_call(functools.partial(finish_kernel, heads), out_shape=outs, i...  1.77 us

profile of v5, /device:TPU:32, one launch (start us, length us, event | category | flops | bytes accessed | tf_op | source)
XLA Modules:
  0.0 73.9 jit_solution(15761355188118403222)
XLA Ops:
  0.6 71.5 %layer.1 = (bf16[128,256]{1,0:T(8,128)(2,1)}, f32[64,1408]{1,0:T(8,128)}) custom-call(bf16[128,2048]{1,0:T(8,128)(2,1)} %refs_0_.1, bf16[2048,256]{1,0:T(8,128)(2,1)} %refs_1_.1, bf16[2048,512]{1,0:T(8,128)(2,1)} %refs_2_.1, bf16[2048,512]{1,0:T(8,128)(2,1)} %refs_3_.1, bf16[4,2048]{1,0:T(4,128)(2,1)} %bitcast.2, bf16[128,256]{1,0:T(8,128)(2,1)} %refs_5_.1), custom_call_target="tpu_custom_call" | custom-call | tf_op jit(solution)/shard_map/layer/pallas_call | solution.py:694
  72.1 1.8 %finish.1 = (bf16[128,256]{1,0:T(8,128)(2,1)}, f32[64,256]{1,0:T(8,128)}, f32[64,512]{1,0:T(8,128)}, f32[64,512]{1,0:T(8,128)}, f32[4,64]{1,0:T(4,128)}) custom-call(bf16[128,256]{1,0:T(8,128)(2,1)} %get-tuple-element.12.gx_in, f32[64,1408]{1,0:T(8,128)} %get-tuple-element.13.gw_in), custom_call_target="tpu_custom_call" | custom-call | tf_op jit(solution)/shard_map/finish/pallas_call | solution.py:710

commit v6 on v5

--- a/solution.py
+++ b/solution.py
@@ -220,6 +220,7 @@
     ]
     r.tt[:, :, own_lanes] = r.tokt[:, x]
 
+    pair_swaps = []
     for h in range(heads):
         maps = [r.ebuf[j, h] for j in range(XN)]
         wide = [m.astype(F32) for m in maps]
@@ -243,14 +244,24 @@
             r.d_off[j, h] = off
             off = off - mm(off, maps[j], NN) + r.blbuf[j, h, quarter:, :].astype(F32)
         r.dz[odd, h] = off.astype(BF16)
-
-    pair_swaps = [
-        start(remote(ref.at[odd], ref.at[odd], r.swap_send.at[i], r.swap_recv.at[i], (beside * XN + x, head)))
-        for i, ref in enumerate((r.fz, r.sz, r.dz))
-    ]
-    for copy in pair_swaps:
-        copy.wait_recv()
-    for h in range(heads):
+        pair_swaps.append(
+            [
+                start(
+                    remote(
+                        ref.at[odd, h],
+                        ref.at[odd, h],
+                        r.swap_send.at[h, i],
+                        r.swap_recv.at[h, i],
+                        (beside * XN + x, head),
+                    )
+                )
+                for i, ref in enumerate((r.fz, r.sz, r.dz))
+            ]
+        )
+
+    for h in range(heads):
+        for copy in pair_swaps[h]:
+            copy.wait_recv()
         low, high = r.fz[0, h], r.fz[1, h]
         both = high.astype(F32) + low.astype(F32) - dg(high, low, NN)
         r.pair[h] = both.astype(BF16)
@@ -266,7 +277,7 @@
         return remote(put.at[peers[i]], got.at[x], r.psend.at[i, kind], r.precv.at[i, kind], row_device(peers[i]))
 
     def hand_out(put, got, kind):
-        for i in range(XN - 1):
+        for i in reversed(range(XN - 1)):
             hand_copy(put, got, kind, i).start()
         got[x] = put[x]
 
@@ -444,6 +455,7 @@
     pad = jnp.zeros((count, size - len(logits)), F32)
     r.g[:, logit_at:] = jnp.concatenate(logits + [pad], axis=1).astype(BF16)
     offer(3)
+    offer(4)
 
     def input_term(d, side):
         lo = pl.multiple_of((lax.rem(y + d, yn) * 2 + side) * block, block)
@@ -523,7 +535,6 @@
     partner_terms()
     relay(1)
     relay(2)
-    offer(4)
     for copy in tok_copies:
         copy.wait_recv()
     ring_step(0, 0)
@@ -674,8 +685,8 @@
         erecv=(heads, 3),
         bsend=(XN - 1,),
         brecv=(XN - 1,),
-        swap_send=(3,),
-        swap_recv=(3,),
+        swap_send=(heads, 3),
+        swap_recv=(heads, 3),
         zsend=(2,),
         zrecv=(2,),
         psend=(XN - 1, 2),

time: 74 us -> 73.2 us (0.989)
  Pallas kernels: 73.3 us -> 72.5 us
    pallas_call x1, Pallas kernels: 71.5 us -> 70.7 us  [per_device(): pl.pallas_call(functools.partial(layer_kernel, zn, yn, heads, names), out...]
where the time goes in v6:
time: 73.2 us; the launch traced here: 73.1 us
  Pallas kernels  72.5 us (99%)
    pallas_call x1, Pallas kernels, per_device(): pl.pallas_call(functools.partial(layer_kernel, zn, yn, heads, names), out...  70.7 us
    pallas_call x1, Pallas kernels, per_device(): pl.pallas_call(functools.partial(finish_kernel, heads), out_shape=outs, i...  1.77 us

profile of v6, /device:TPU:32, one launch (start us, length us, event | category | flops | bytes accessed | tf_op | source)
XLA Modules:
  0.0 73.1 jit_solution(14203377417320011575)
XLA Ops:
  0.6 70.7 %layer.1 = (bf16[128,256]{1,0:T(8,128)(2,1)}, f32[64,1408]{1,0:T(8,128)}) custom-call(bf16[128,2048]{1,0:T(8,128)(2,1)} %refs_0_.1, bf16[2048,256]{1,0:T(8,128)(2,1)} %refs_1_.1, bf16[2048,512]{1,0:T(8,128)(2,1)} %refs_2_.1, bf16[2048,512]{1,0:T(8,128)(2,1)} %refs_3_.1, bf16[4,2048]{1,0:T(4,128)(2,1)} %bitcast.2, bf16[128,256]{1,0:T(8,128)(2,1)} %refs_5_.1), custom_call_target="tpu_custom_call" | custom-call | tf_op jit(solution)/shard_map/layer/pallas_call | solution.py:705
  71.4 1.8 %finish.1 = (bf16[128,256]{1,0:T(8,128)(2,1)}, f32[64,256]{1,0:T(8,128)}, f32[64,512]{1,0:T(8,128)}, f32[64,512]{1,0:T(8,128)}, f32[4,64]{1,0:T(4,128)}) custom-call(bf16[128,256]{1,0:T(8,128)(2,1)} %get-tuple-element.12.gx_in, f32[64,1408]{1,0:T(8,128)} %get-tuple-element.13.gw_in), custom_call_target="tpu_custom_call" | custom-call | tf_op jit(solution)/shard_map/finish/pallas_call | solution.py:721

commit v7 on v6

--- a/solution.py
+++ b/solution.py
@@ -538,11 +538,11 @@
     for copy in tok_copies:
         copy.wait_recv()
     ring_step(0, 0)
-    own_terms()
     relay(3)
     ring_step(1, 0)
     ring_step(2, 0)
     relay(4)
+    own_terms()
     for p in (0, 1, 2):
         ring_step(p, 1)
     ring_step(3, 0)

time: 73.2 us -> 73 us (level)
  no operation moved by 1% of the time
where the time goes in v7:
time: 73 us; the launch traced here: 72.9 us
  Pallas kernels  72.3 us (99%)
    pallas_call x1, Pallas kernels, per_device(): pl.pallas_call(functools.partial(layer_kernel, zn, yn, heads, names), out...  70.5 us
    pallas_call x1, Pallas kernels, per_device(): pl.pallas_call(functools.partial(finish_kernel, heads), out_shape=outs, i...  1.77 us

profile of v7, /device:TPU:32, one launch (start us, length us, event | category | flops | bytes accessed | tf_op | source)
XLA Modules:
  0.0 72.9 jit_solution(5123536993859563198)
XLA Ops:
  0.6 70.5 %layer.1 = (bf16[128,256]{1,0:T(8,128)(2,1)}, f32[64,1408]{1,0:T(8,128)}) custom-call(bf16[128,2048]{1,0:T(8,128)(2,1)} %refs_0_.1, bf16[2048,256]{1,0:T(8,128)(2,1)} %refs_1_.1, bf16[2048,512]{1,0:T(8,128)(2,1)} %refs_2_.1, bf16[2048,512]{1,0:T(8,128)(2,1)} %refs_3_.1, bf16[4,2048]{1,0:T(4,128)(2,1)} %bitcast.2, bf16[128,256]{1,0:T(8,128)(2,1)} %refs_5_.1), custom_call_target="tpu_custom_call" | custom-call | tf_op jit(solution)/shard_map/layer/pallas_call | solution.py:705
  71.1 1.8 %finish.1 = (bf16[128,256]{1,0:T(8,128)(2,1)}, f32[64,256]{1,0:T(8,128)}, f32[64,512]{1,0:T(8,128)}, f32[64,512]{1,0:T(8,128)}, f32[4,64]{1,0:T(4,128)}) custom-call(bf16[128,256]{1,0:T(8,128)(2,1)} %get-tuple-element.12.gx_in, f32[64,1408]{1,0:T(8,128)} %get-tuple-element.13.gw_in), custom_call_target="tpu_custom_call" | custom-call | tf_op jit(solution)/shard_map/finish/pallas_call | solution.py:721

commit v8 on v7

--- a/solution.py
+++ b/solution.py
@@ -186,7 +186,7 @@
             r.bl_own[j, h, quarter:, :] = adjoint[j * quarter : (j + 1) * quarter].astype(BF16)
     bl_copies = [
         start(remote(r.bl_own.at[peer], r.blbuf.at[x], r.bsend.at[i], r.brecv.at[i], row_device(peer)))
-        for i, peer in enumerate(peers)
+        for i, peer in reversed(list(enumerate(peers)))
     ]
     r.ebuf[x] = r.e_own[...]
     r.blbuf[x] = r.bl_own[x]

time: 73 us -> 73.1 us (level)
  no operation moved by 1% of the time
where the time goes in v8:
time: 73.1 us; the launch traced here: 73 us
  Pallas kernels  72.4 us (99%)
    pallas_call x1, Pallas kernels, per_device(): pl.pallas_call(functools.partial(layer_kernel, zn, yn, heads, names), out...  70.6 us
    pallas_call x1, Pallas kernels, per_device(): pl.pallas_call(functools.partial(finish_kernel, heads), out_shape=outs, i...  1.77 us

profile of v8, /device:TPU:32, one launch (start us, length us, event | category | flops | bytes accessed | tf_op | source)
XLA Modules:
  0.0 73.0 jit_solution(10813662579437812496)
XLA Ops:
  0.6 70.6 %layer.1 = (bf16[128,256]{1,0:T(8,128)(2,1)}, f32[64,1408]{1,0:T(8,128)}) custom-call(bf16[128,2048]{1,0:T(8,128)(2,1)} %refs_0_.1, bf16[2048,256]{1,0:T(8,128)(2,1)} %refs_1_.1, bf16[2048,512]{1,0:T(8,128)(2,1)} %refs_2_.1, bf16[2048,512]{1,0:T(8,128)(2,1)} %refs_3_.1, bf16[4,2048]{1,0:T(4,128)(2,1)} %bitcast.2, bf16[128,256]{1,0:T(8,128)(2,1)} %refs_5_.1), custom_call_target="tpu_custom_call" | custom-call | tf_op jit(solution)/shard_map/layer/pallas_call | solution.py:705
  71.2 1.8 %finish.1 = (bf16[128,256]{1,0:T(8,128)(2,1)}, f32[64,256]{1,0:T(8,128)}, f32[64,512]{1,0:T(8,128)}, f32[64,512]{1,0:T(8,128)}, f32[4,64]{1,0:T(4,128)}) custom-call(bf16[128,256]{1,0:T(8,128)(2,1)} %get-tuple-element.12.gx_in, f32[64,1408]{1,0:T(8,128)} %get-tuple-element.13.gw_in), custom_call_target="tpu_custom_call" | custom-call | tf_op jit(solution)/shard_map/finish/pallas_call | solution.py:721
